TPU v7x, 128 devices: a whole 4x4x4 slice. The times are simulated.
128 devices in a mesh: req: 16 (over y, z), mlp: 8 (over x, core).
Axes of the slice: x: 4, y: 4, z: 4, core: 2. Of those that a mesh axis runs over, the one named last changes fastest.
Arguments:
- blocks: bfloat16 [2048, 4096], P('req'), may hold values from -6 to 6
- token_embed: bfloat16 [2048, 4096], P('req'), may hold values from -6 to 6
- accepted: int32 [2048], P('req'), may hold values 0 or 1
- prompt_len: int32 [16], P('req'), may hold values from 2 to 512, as said below
- cache_len: int32 [16, 8], P('req'), may hold values from 1 to 1024, as said below
- prompt_kv: bfloat16 [16, 512, 2048], P('req', None, 'mlp'), may hold values from -364 to 364
- cache_kv: bfloat16 [16, 8, 1024, 2048], P('req', None, None, 'mlp'), may hold values from -6 to 6
- attn_gain: float32 [4096], replicated, may hold values from 0.25 to 1.75
- w_q: bfloat16 [4096, 4096], P(None, 'mlp'), may hold values from -0.09375 to 0.09375
- w_kv: bfloat16 [4096, 2048], P(None, 'mlp'), may hold values from -0.09375 to 0.09375
- w_o: bfloat16 [4096, 4096], P('mlp'), may hold values from -0.09375 to 0.09375
- mlp_gain: float32 [4096], replicated, may hold values from 0.25 to 1.75
- w_gate: bfloat16 [4096, 7168], P('req', 'mlp'), may hold values from -0.09375 to 0.09375
- w_up: bfloat16 [4096, 7168], P('req', 'mlp'), may hold values from -0.09375 to 0.09375
- w_down: bfloat16 [7168, 4096], P('mlp'), may hold values from -0.0625 to 0.0625
Outputs:
- denoised: bfloat16 [2048, 4096], P('req')
Inputs may be any that keep to these rules, and one draw needn't show every extreme that they name: `prompt_len`: shared by the 8 requests of a group; some group has a prompt of exactly 512. `cache_len`: every group has a request with exactly 1024 cached tokens.
All inputs are finite; a program needn't handle non-finite values. No bound on the sum of `accepted` on one device may be relied on, other than what follows from the above.
Results may differ from a plain program's by a relative error of at most 0.022.
Values may be sent and summed in bfloat16 or wider, within the bound.
A program may use at most 128 MiB of HBM per device.

v0:
```python
import math

import jax
import jax.numpy as jnp
from jax import lax
from jax.sharding import PartitionSpec as P

HEAD_DIM = 128
REQS = 8
BLOCK = 16


EPSILON = 1e-05
THETA = 500000.0


def rms_scale(stream, gain):
    widened = stream.astype(jnp.float32)
    mean_square = jnp.mean(widened * widened, axis=-1, keepdims=True)
    return (widened * lax.rsqrt(mean_square + EPSILON) * gain).astype(jnp.bfloat16)


def rope(values, positions):
    head_size = values.shape[-1]
    half_size = head_size // 2
    frequency = THETA ** (-2.0 * jnp.arange(half_size, dtype=jnp.float32) / head_size)
    angles = positions.astype(jnp.float32)[:, None] * frequency[None, :]
    cosine = jnp.cos(angles)[:, None, :]
    sine = jnp.sin(angles)[:, None, :]
    first = values[..., :half_size]
    second = values[..., half_size:]
    return jnp.concatenate(
        [first * cosine - second * sine, second * cosine + first * sine], axis=-1
    )


def attend_one(
    queries, block_keys, block_values, prompt_part, cached_part, prompt_size, cache_size
):
    block_len, head_count, head_size = queries.shape
    kv_heads = block_keys.shape[1]
    group_size = head_count // kv_heads
    grouped = queries.reshape(block_len, kv_heads, group_size, head_size)
    scale = 1.0 / math.sqrt(head_size)

    def scores(keys):
        return (
            jnp.einsum("tkgd,lkd->kgtl", grouped, keys, preferred_element_type=jnp.float32) * scale
        )

    prompt_score = scores(prompt_part[:, :, 0])
    cache_score = scores(cached_part[:, :, 0])
    block_score = scores(block_keys)
    prompt_ok = jnp.arange(prompt_part.shape[0], dtype=jnp.int32) < prompt_size
    cache_ok = jnp.arange(cached_part.shape[0], dtype=jnp.int32) < cache_size
    prompt_score = jnp.where(prompt_ok, prompt_score, -1e30)
    cache_score = jnp.where(cache_ok, cache_score, -1e30)
    largest = jnp.maximum(
        jnp.maximum(
            jnp.max(prompt_score, -1, keepdims=True), jnp.max(cache_score, -1, keepdims=True)
        ),
        jnp.max(block_score, -1, keepdims=True),
    )
    prompt_exp = jnp.exp(prompt_score - largest)
    cache_exp = jnp.exp(cache_score - largest)
    block_exp = jnp.exp(block_score - largest)
    total = (
        jnp.sum(prompt_exp, -1, keepdims=True)
        + jnp.sum(cache_exp, -1, keepdims=True)
        + jnp.sum(block_exp, -1, keepdims=True)
    )
    prompt_w = (prompt_exp / total).astype(jnp.bfloat16)
    cache_w = (cache_exp / total).astype(jnp.bfloat16)
    block_w = (block_exp / total).astype(jnp.bfloat16)
    result = jnp.einsum(
        "kgtl,lkd->tkgd", prompt_w, prompt_part[:, :, 1], preferred_element_type=jnp.float32
    )
    result = result + jnp.einsum(
        "kgtl,lkd->tkgd", cache_w, cached_part[:, :, 1], preferred_element_type=jnp.float32
    )
    result = result + jnp.einsum(
        "kgtl,lkd->tkgd", block_w, block_values, preferred_element_type=jnp.float32
    )
    return result.reshape(block_len, head_count * head_size).astype(jnp.bfloat16)


def swiglu(gate, up_part):
    return (jax.nn.silu(gate) * up_part).astype(jnp.bfloat16)


def body(
    blocks,
    token_embed,
    accepted,
    prompt_len,
    cache_len,
    prompt_kv,
    cache_kv,
    attn_gain,
    w_q,
    w_kv,
    w_o,
    mlp_gain,
    w_gate,
    w_up,
    w_down,
):
    row_count = blocks.shape[0]
    prompt_size = prompt_len[0]
    cache_sizes = cache_len[0]
    positions = (
        prompt_size + cache_sizes[:, None] + jnp.arange(BLOCK, dtype=jnp.int32)[None, :]
    ).reshape(-1)
    local_kv = w_kv.shape[1] // (2 * HEAD_DIM)
    local_heads = w_q.shape[1] // HEAD_DIM
    prompt_part = prompt_kv[0].reshape(-1, local_kv, 2, HEAD_DIM)
    cached = cache_kv[0].reshape(REQS, -1, local_kv, 2, HEAD_DIM)

    def one_pass(stream):
        normed = rms_scale(stream, attn_gain)
        queries = rope(
            jnp.dot(normed, w_q, preferred_element_type=jnp.float32).reshape(
                row_count, local_heads, HEAD_DIM
            ),
            positions,
        ).astype(jnp.bfloat16)
        key_value = jnp.dot(normed, w_kv, preferred_element_type=jnp.float32).reshape(
            row_count, local_kv, 2, HEAD_DIM
        )
        keys = rope(key_value[:, :, 0], positions).astype(jnp.bfloat16)
        values = key_value[:, :, 1].astype(jnp.bfloat16)

        def attend_request(items):
            query_part, key_part, value_part, cache_part, cache_size = items
            return attend_one(
                query_part, key_part, value_part, prompt_part, cache_part, prompt_size, cache_size
            )

        attended = lax.map(
            attend_request,
            (
                queries.reshape(REQS, BLOCK, local_heads, HEAD_DIM),
                keys.reshape(REQS, BLOCK, local_kv, HEAD_DIM),
                values.reshape(REQS, BLOCK, local_kv, HEAD_DIM),
                cached,
                cache_sizes,
            ),
        )
        attended = attended.reshape(row_count, local_heads * HEAD_DIM)
        mixed = lax.psum(jnp.dot(attended, w_o, preferred_element_type=jnp.float32), "mlp")
        after_attn = (stream.astype(jnp.float32) + mixed).astype(jnp.bfloat16)
        normed2 = rms_scale(after_attn, mlp_gain)
        pass_gate, pass_up = (
            lax.all_gather(w_gate, "req", axis=0, tiled=True),
            lax.all_gather(w_up, "req", axis=0, tiled=True),
        )
        gate = jnp.dot(normed2, pass_gate, preferred_element_type=jnp.float32)
        up_part = jnp.dot(normed2, pass_up, preferred_element_type=jnp.float32)
        hidden = swiglu(gate, up_part)
        down = lax.psum(jnp.dot(hidden, w_down, preferred_element_type=jnp.float32), "mlp")
        return (after_attn.astype(jnp.float32) + down).astype(jnp.bfloat16)

    first = one_pass(blocks)
    second_input = jnp.where(accepted[:, None] == 1, token_embed, first)
    return one_pass(second_input)


def solution(mesh):
    return jax.shard_map(
        body,
        mesh=mesh,
        in_specs=(
            P("req", None),
            P("req", None),
            P("req"),
            P("req"),
            P("req", None),
            P("req", None, "mlp"),
            P("req", None, None, "mlp"),
            P(),
            P(None, "mlp"),
            P(None, "mlp"),
            P("mlp", None),
            P(),
            P("req", "mlp"),
            P("req", "mlp"),
            P("mlp", None),
        ),
        out_specs=P("req", None),
        check_vma=False,
    )
```

profile of v0, /device:TPU:1, one launch (start us, length us, event | category | flops | bytes accessed | tf_op | source)
XLA Modules:
  0.0 503.6 jit_solution(11946350769607813790)
XLA Ops:
  7.4 1.7 fusion.76
  9.3 1.8 fusion.119
  12.8 2.9 fusion.121
  17.3 1.4 copy.63
  18.8 6.4 %copy.26 = bf16[1,8,1024,256]{2,3,1,0:T(8,128)(2,1)} copy(bf16[1,8,1024,256]{3,2,1,0:T(8,128)(2,1)} %param.25) | data formatting | bytes 8388608 | tf_op args[6]
  25.2 6.5 %copy.30 = bf16[8,1024,1,2,128]{4,1,3,2,0:T(8,128)(2,1)} copy(bf16[8,1024,1,2,128]{1,4,3,0,2:T(8,128)(2,1)} %bitcast.294) | data formatting | bytes 8388608 | tf_op jit(solution)/shard_map/while | solution.py:139
  33.1 45.7 %while.20 = (s32[]{:T(128)}, bf16[8,16,512]{2,1,0:T(8,128)(2,1)S(1)}, s32[]{:T(128)}, bf16[8,16,4,128]{3,1,0,2:T(8,128)(2,1)S(1)}, bf16[512,1,2,128]{3,0,2,1:T(8...) while((s32[]{:T(128)}, ...), condition=%wide.region_8.9_spmd, body=%wide.region_1.8_spmd.sunk | while | flops 51675520 | bytes 3347849 | solution.py:139
  78.8 4.2 fusion.154
  84.3 67.0 %all-reduce.5.cloned.1.call-done = f32[128,4096]{1,0:T(8,128)} async-done(((f32[128,4096]{1,0:T(8,128)}), f32[128,4096]{1,0:T(8,128)}) %all-reduce.5.cloned.1.call-update) | async-done | bytes 2097168 | tf_op jit(solution)/shard_map/psum | solution.py:150
  151.2 2.3 fusion.80
  155.2 5.2 %fusion.117 = f32[128,896]{1,0:T(8,128)} fusion(bf16[4096,896]{1,0:T(8,128)(2,1)} %all-gather.3.cloned.1.call-done, bf16[128,4096]{1,0:T(8,128)(2,1)S(1)} %get-tuple-element.160, f32[4096]{0:T(1024)S(1)} %copy-done.6, f32[128]{0:T(128)} %add_rsqrt_fusion.2), kind=kOutput, calls=%fused_computation.162 | convolution fusion | flops 941621248 | bytes 8864256 | tf_op jit(solution)/shard_map/dot_general | solution.py:157
  160.3 62.8 %all-gather.5.cloned.1.call-done = bf16[4096,896]{1,0:T(8,128)(2,1)} async-done(((bf16[256,896]{1,0:T(8,128)(2,1)}), bf16[4096,896]{1,0:T(8,128)(2,1)}) %all-gather.5.cloned.1.call-update) | async-done | bytes 7340048 | tf_op jit(solution)/shard_map/all_gather | solution.py:155
  223.1 9.0 %fusion.96 = f32[128,4096]{1,0:T(8,128)} fusion(bf16[896,4096]{1,0:T(8,128)(2,1)} %param.33, bf16[4096,896]{1,0:T(8,128)(2,1)} %all-gather.5.cloned.1.call-done, f32[128,896]{1,0:T(8,128)} %fusion.117, bf16[128,4096]{1,0:T(8,128)(2,1)S(1)} %get-tuple-element.160, f32[4096]{0:T(1024)S(1)} %copy-done.6, f32[128]{0:T(128)} %add_rsqrt_fusion.2), kind=kOutput, calls=%fused_computation.148 | convolution fusion | flops 1881833472 | bytes 18301440 | tf_op jit(solution)/shard_map/dot_general | solution.py:160
  233.6 62.1 %all-reduce.7.cloned.1.call-done = f32[128,4096]{1,0:T(8,128)} async-done(((f32[128,4096]{1,0:T(8,128)}), f32[128,4096]{1,0:T(8,128)}) %all-reduce.7.cloned.1.call-update) | async-done | bytes 2097168 | tf_op jit(solution)/shard_map/psum | solution.py:160
  295.7 2.5 fusion.84
  299.9 3.3 fusion.113
  304.2 39.2 %while.21 = (s32[]{:T(128)}, bf16[8,16,512]{2,1,0:T(8,128)(2,1)S(1)}, s32[]{:T(128)}, bf16[8,16,4,128]{3,1,0,2:T(8,128)(2,1)S(1)}, bf16[512,1,2,128]{3,0,2,1:T(8...) while((s32[]{:T(128)}, ...), condition=%wide.region_20.21_spmd, body=%wide.region_13.20_spmd.sunk | while | flops 51675520 | bytes 3379597 | solution.py:139
  343.4 4.3 fusion.155
  347.7 65.2 %all-reduce.9.cloned.1.call-done = f32[128,4096]{1,0:T(8,128)} async-done(((f32[128,4096]{1,0:T(8,128)}), f32[128,4096]{1,0:T(8,128)}) %all-reduce.9.cloned.1.call-update) | async-done | bytes 2097168 | tf_op jit(solution)/shard_map/psum | solution.py:150
  413.0 2.0 fusion.88
  415.0 4.4 fusion.109
  419.4 9.0 %fusion.95 = f32[128,4096]{1,0:T(8,128)} fusion(bf16[896,4096]{1,0:T(8,128)(2,1)} %param.33, bf16[4096,896]{1,0:T(8,128)(2,1)} %all-gather.5.cloned.1.call-done, f32[128,896]{1,0:T(8,128)S(1)} %fusion.109, bf16[128,4096]{1,0:T(8,128)(2,1)S(1)} %get-tuple-element.156, f32[128]{0:T(128)S(1)} %add_rsqrt_fusion, f32[4096]{0:T(1024)S(1)} %copy-done.6), kind=kOutput, calls=%fused_computation.147 | convolution fusion | flops 1881833472 | bytes 18301440 | tf_op jit(solution)/shard_map/dot_general | solution.py:160
  428.4 65.3 %all-reduce.11.cloned.1.call-done = f32[128,4096]{1,0:T(8,128)} async-done(((f32[128,4096]{1,0:T(8,128)}), f32[128,4096]{1,0:T(8,128)}) %all-reduce.11.cloned.1.call-update) | async-done | bytes 2097168 | tf_op jit(solution)/shard_map/psum | solution.py:160
  493.7 2.8 fusion.91
  (368 shorter events, 94.7 us)
Async XLA Ops:
  7.4 1.9 copy-start
  7.4 143.9 %all-reduce.5.cloned.1.call-start = ((), (), s32[]{:S(2)}) async-start(), calls=%async_computation | async-start | bytes 4194304 | tf_op jit(solution)/shard_map/psum | solution.py:150
  7.4 9.0 %copy-start.9 = (f32[64]{0:T(128)}, f32[64]{0:T(128)S(1)}, u32[]{:S(2)}) copy-start(f32[64]{0:T(128)S(1)} %multiply_power_fusion) | copy-start | bytes 772
  9.3 3.3 copy-start.14
  9.3 3.5 copy-start.2
  9.3 3.5 copy-start.11
  12.8 3.6 copy-start.7
  25.2 6.5 %copy-start.5 = (bf16[1,512,256]{2,1,0:T(8,128)(2,1)S(1)}, bf16[1,512,256]{2,1,0:T(8,128)(2,1)}, u32[]{:S(2)}) copy-start(bf16[1,512,256]{2,1,0:T(8,128)(2,1)} %param.24) | copy-start | bytes 786436
  83.0 72.1 %all-gather.3.cloned.1.call-start = ((), (), s32[]{:S(2)}) async-start(), calls=%async_computation.1 | async-start | bytes 7798784 | tf_op jit(solution)/shard_map/all_gather | solution.py:154
  83.6 139.5 %all-gather.5.cloned.1.call-start = ((), (), s32[]{:S(2)}) async-start(), calls=%async_computation.2 | async-start | bytes 7798784 | tf_op jit(solution)/shard_map/all_gather | solution.py:155
  84.2 70.9 %copy-start.6 = (f32[4096]{0:T(1024)S(1)}, f32[4096]{0:T(1024)}, u32[]{:S(2)}) copy-start(f32[4096]{0:T(1024)} %param.30) | copy-start | bytes 49156
  84.2 211.5 %all-reduce.7.cloned.1.call-start = ((), (), s32[]{:S(2)}) async-start(), calls=%async_computation.3 | async-start | bytes 4194304 | tf_op jit(solution)/shard_map/psum | solution.py:160
  232.2 180.8 %all-reduce.9.cloned.1.call-start = ((), (), s32[]{:S(2)}) async-start(), calls=%async_computation.4 | async-start | bytes 4194304 | tf_op jit(solution)/shard_map/psum | solution.py:150
  295.7 3.5 copy-start.12
  298.2 1.0 copy-start.3
  299.2 0.7 copy-start.13
  299.9 3.3 copy-start.8
  299.9 3.3 copy-start.10
  303.2 1.0 copy-start.15
  347.7 65.3 %copy-start.4 = (bf16[128,4096]{1,0:T(8,128)(2,1)S(1)}, bf16[128,4096]{1,0:T(8,128)(2,1)}, u32[]{:S(2)}) copy-start(bf16[128,4096]{1,0:T(8,128)(2,1)} %copy-done.3) | copy-start | bytes 3145732
  347.7 146.0 %all-reduce.11.cloned.1.call-start = ((), (), s32[]{:S(2)}) async-start(), calls=%async_computation.5 | async-start | bytes 4194304 | tf_op jit(solution)/shard_map/psum | solution.py:160
  428.4 68.1 %copy-start.1 = (bf16[4096,256]{1,0:T(8,128)(2,1)S(1)}, bf16[4096,256]{1,0:T(8,128)(2,1)}, u32[]{:S(2)}) copy-start(bf16[4096,256]{1,0:T(8,128)(2,1)} %param.28) | copy-start | bytes 6291460
Sparse Core Ops, SparseCore 0:
  83.2 68.0 all-reduce.4
  232.3 63.3 all-reduce.6
  347.8 65.1 all-reduce.8
  428.5 65.1 all-reduce.10
Sparse Core Ops, SparseCore 1:
  85.7 69.4 all-gather.2
  157.2 65.9 all-gather.4
where the time goes:
time: 507 us; the launch traced here: 504 us
  waiting for transfers between devices  325 us (64%)
  matrix products  72.5 us (14%)
  local copies, waits for them, and re-layouts  45.8 us (9%)
  other arithmetic  43.5 us (9%)
  between operations  15.6 us (3%)
    psum x2, waiting for transfers between devices, one_pass(): lax.psum(jnp.dot(attended, w_o, preferred_element_type=jnp.float32), 'mlp')  132 us
    psum x2, waiting for transfers between devices, one_pass(): lax.psum(jnp.dot(hidden, w_down, preferred_element_type=jnp.float32), 'mlp')  127 us
    all_gather x1, waiting for transfers between devices, one_pass(): lax.all_gather(w_up, 'req', axis=0, tiled=True)  62.8 us
    dot_general x2, matrix products, one_pass(): jnp.dot(hidden, w_down, preferred_element_type=jnp.float32)  18 us
    squeeze x16, local copies, waits for them, and re-layouts, one_pass(): lax.map(attend_request, (queries.reshape(REQS, BLOCK, local_heads, HEAD_D...  17.3 us
    dot_general x48, matrix products, scores(): jnp.einsum('tkgd,lkd->kgtl', grouped, keys, preferred_element_type=jnp.fl...  11.7 us
    lt x16, other arithmetic, attend_one(): prompt_ok = jnp.arange(prompt_part.shape[0], dtype=jnp.int32) < prompt_size  10.5 us
    lt x16, other arithmetic, attend_one(): cache_ok = jnp.arange(cached_part.shape[0], dtype=jnp.int32) < cache_size  10.4 us
  transfers between devices with their start and end apart: 6, of which 6 were waited for; matrix products, arithmetic and copies ran while one was open for 2% of the time, Pallas kernels for 0%

commit v1 on v0

v1 whole, which is shorter than its diff:
```python
import functools
import math

import jax
import jax.numpy as jnp
from jax import lax
from jax.experimental import pallas as pl
from jax.experimental.pallas import tpu as pltpu
from jax.sharding import PartitionSpec as P

D = 4096
HEAD_DIM = 128
HEADS = 4
REQS = 8
BLOCK = 16
ROWS = REQS * BLOCK
CACHE = 1024
PMAX = 512
HIDDEN = 896
SHARD = 256
OWN = 16
EPSILON = 1e-05
THETA = 500000.0
MESH = pl.DeviceIdType.MESH
N_RS = 4
RS_W = D // N_RS
N_AG = 2
AG_W = D // N_AG
F32 = jnp.float32
BF16 = jnp.bfloat16


def kernel(
    lens, cos, sin, accepted, attn_gain, mlp_gain,
    blocks, token, prompt, cache, w_q, w_kv, w_o, w_gate, w_up, w_down,
    out,
    x_v, tok_v, prm_v, cache_v, wq_v, wkv_v, wo_v, gate_v, up_v, wd_v,
    nrm, qkv, q_s, k_s, v_s, att, g_acc, u_acc, hid,
    part, sib_out, sib_in, x_out, x_in, res,
    load_sem, g_send, g_recv, sib_ss, sib_rs, x_ss, x_rs, agx_s, agx_r, ags_s, ags_r,
):
    r = lax.axis_index("req")
    m = lax.axis_index("mlp")
    y, z = lax.div(r, 4), lax.rem(r, 4)
    x, c = lax.div(m, 2), lax.rem(m, 2)

    def add4(v, d):
        return lax.rem(v + (d % 4), 4)

    def chip(d):
        return (r, add4(x, d) * 2 + c)

    sibling = (r, x * 2 + 1 - c)

    def plane(dy, dz):
        return (add4(y, dy) * 4 + add4(z, dz), m)

    my_half = pl.multiple_of(64 * c, 64)
    other_half = pl.multiple_of(64 * (1 - c), 64)
    my_rows = pl.multiple_of(64 * c + OWN * x, OWN)

    own_shard = pl.ds(pl.multiple_of(r * SHARD, SHARD), SHARD)
    loads = {}
    for i, (name, src, dst) in enumerate(
        [
            ("gate", w_gate, gate_v.at[own_shard]),
            ("up", w_up, up_v.at[own_shard]),
            ("blocks", blocks, x_v),
            ("wq", w_q, wq_v),
            ("wkv", w_kv, wkv_v),
            ("prompt", prompt, prm_v),
            ("cache", cache, cache_v),
            ("wo", w_o, wo_v),
            ("wd", w_down, wd_v),
            ("tok", token.at[pl.ds(my_rows, OWN)], tok_v),
        ]
    ):
        copy = pltpu.make_async_copy(src, dst, load_sem.at[i])
        copy.start()
        loads[name] = copy

    barrier = pltpu.get_barrier_semaphore()
    partners = [chip(1), chip(2), chip(3), sibling, plane(0, 1), plane(0, 3), plane(1, 0), plane(3, 0)]
    for who in partners:
        pl.semaphore_signal(barrier, inc=1, device_id=who, device_id_type=MESH)
    pl.semaphore_wait(barrier, len(partners))

    full = (gate_v, up_v)
    sends = ([], [])

    def index(mat, a, b):
        dy, dz = (b, a) if mat == 0 else (a, b)
        return add4(y, dy) * 4 + add4(z, dz)

    def piece(mat, a, b, half):
        start = index(mat, a, b) * SHARD
        if half is None:
            return full[mat].at[pl.ds(pl.multiple_of(start, SHARD), SHARD)]
        return full[mat].at[pl.ds(pl.multiple_of(start + half * (SHARD // 2), SHARD // 2), SHARD // 2)]

    def g_copy(mat, a, b, half, axis, step, send_sem):
        da, db = (step, 0) if axis == 0 else (0, step)
        dy, dz = (db, da) if mat == 0 else (da, db)
        ref = piece(mat, a, b, half)
        return pltpu.make_async_remote_copy(
            src_ref=ref,
            dst_ref=ref,
            send_sem=send_sem,
            recv_sem=g_recv.at[mat, (a - da) % 4, (b - db) % 4, half or 0],
            device_id=plane(dy, dz),
            device_id_type=MESH,
        )

    def g_start(mat, a, b, half, axis, step):
        copy = g_copy(mat, a, b, half, axis, step, g_send.at[mat, len(sends[mat])])
        copy.start()
        sends[mat].append(copy)

    def g_wait(mat, a, b, half=None):
        ref = piece(mat, a, b, half)
        pltpu.make_async_remote_copy(
            src_ref=ref,
            dst_ref=ref,
            send_sem=g_send.at[mat, 0],
            recv_sem=g_recv.at[mat, a % 4, b % 4, half or 0],
            device_id=plane(0, 1),
            device_id_type=MESH,
        ).wait_recv()

    def gather_0():
        loads["gate"].wait()
        loads["up"].wait()
        for axis in (0, 1):
            for mat in (0, 1):
                g_start(mat, 0, 0, None, axis, 1)
                g_start(mat, 0, 0, None, axis, -1)

    def gather_1():
        for mat in (0, 1):
            g_wait(mat, -1, 0)
            g_start(mat, -1, 0, 0, 0, 1)
            g_wait(mat, 1, 0)
            g_start(mat, 1, 0, 1, 0, -1)
        for a in (-1, 1):
            for mat in (0, 1):
                g_start(mat, a, 0, None, 1, 1)
                g_start(mat, a, 0, None, 1, -1)

    def forward(a):
        for mat in (0, 1):
            g_wait(mat, a, -1)
            g_start(mat, a, -1, 0, 1, 1)
            g_wait(mat, a, 1)
            g_start(mat, a, 1, 1, 1, -1)

    def gather_3():
        for mat in (0, 1):
            g_wait(mat, 2, 0, 0)
            g_wait(mat, 2, 0, 1)
            g_start(mat, 2, 0, None, 1, 1)
            g_start(mat, 2, 0, None, 1, -1)

    def norm_local():
        def step(i, carry):
            rows = pl.ds(pl.multiple_of(i * OWN, OWN), OWN)
            wide = x_v[rows, :].astype(F32)
            scale = lax.rsqrt(jnp.mean(wide * wide, axis=-1, keepdims=True) + EPSILON)
            nrm[rows, :] = (wide * scale * attn_gain[...]).astype(BF16)
            return carry

        lax.fori_loop(0, ROWS // OWN, step, 0)

    def project(ready):
        for k in range(N_AG):
            ready(k)
            cols = slice(k * AG_W, (k + 1) * AG_W)
            lhs = nrm[:, cols]
            q_part = jnp.dot(lhs, wq_v[cols, :], preferred_element_type=F32)
            kv_part = jnp.dot(lhs, wkv_v[cols, :], preferred_element_type=F32)
            if k == 0:
                qkv[:, : HEADS * HEAD_DIM] = q_part
                qkv[:, HEADS * HEAD_DIM :] = kv_part
            else:
                qkv[:, : HEADS * HEAD_DIM] += q_part
                qkv[:, HEADS * HEAD_DIM :] += kv_part

    def attention():
        def rope(values):
            return (values * cos[...] + pltpu.roll(values, HEAD_DIM // 2, 1) * sin[...]).astype(BF16)

        for h in range(HEADS):
            q_s[:, BLOCK * h : BLOCK * (h + 1), :] = rope(
                qkv[:, HEAD_DIM * h : HEAD_DIM * (h + 1)]
            ).reshape(REQS, BLOCK, HEAD_DIM)
        base = HEADS * HEAD_DIM
        k_s[...] = rope(qkv[:, base : base + HEAD_DIM]).reshape(REQS, BLOCK, HEAD_DIM)
        v_s[...] = qkv[:, base + HEAD_DIM :].astype(BF16).reshape(REQS, BLOCK, HEAD_DIM)
        scale = 1.0 / math.sqrt(HEAD_DIM)
        contract = (((1,), (1,)), ((), ()))

        def step(j, carry):
            q = q_s[j]

            def scores(keys):
                return lax.dot_general(q, keys, contract, preferred_element_type=F32) * scale

            s_c = scores(cache_v[j, :, :HEAD_DIM])
            s_p = scores(prm_v[:, :HEAD_DIM])
            s_b = scores(k_s[j])
            at_c = lax.broadcasted_iota(jnp.int32, s_c.shape, 1)
            at_p = lax.broadcasted_iota(jnp.int32, s_p.shape, 1)
            s_c = jnp.where(at_c < lens[1 + j], s_c, -1e30)
            s_p = jnp.where(at_p < lens[0], s_p, -1e30)
            top = jnp.maximum(
                jnp.maximum(jnp.max(s_c, -1, keepdims=True), jnp.max(s_p, -1, keepdims=True)),
                jnp.max(s_b, -1, keepdims=True),
            )
            e_c = jnp.exp(s_c - top)
            e_p = jnp.exp(s_p - top)
            e_b = jnp.exp(s_b - top)
            total = (
                jnp.sum(e_c, -1, keepdims=True)
                + jnp.sum(e_p, -1, keepdims=True)
                + jnp.sum(e_b, -1, keepdims=True)
            )
            mixed = jnp.dot(e_c.astype(BF16), cache_v[j, :, HEAD_DIM:], preferred_element_type=F32)
            mixed += jnp.dot(e_p.astype(BF16), prm_v[:, HEAD_DIM:], preferred_element_type=F32)
            mixed += jnp.dot(e_b.astype(BF16), v_s[j], preferred_element_type=F32)
            mixed = (mixed / total).astype(BF16)
            for h in range(HEADS):
                att[j, :, HEAD_DIM * h : HEAD_DIM * (h + 1)] = mixed[BLOCK * h : BLOCK * (h + 1)]
            return carry

        lax.fori_loop(0, REQS, step, 0)

    pending = []

    def reduce_scatter(lhs, weight):
        def chips(n):
            sib_copies[n].wait_recv()
            total = part[n, pl.ds(my_half, 64), :] + sib_in[n].astype(F32)
            part[n, pl.ds(my_half, 64), :] = total
            x_out[n] = total.astype(BF16).reshape(4, OWN, RS_W)
            for d in (2, 1, 3):
                copy = pltpu.make_async_remote_copy(
                    src_ref=x_out.at[n, add4(x, d)],
                    dst_ref=x_in.at[n, d],
                    send_sem=x_ss.at[n, d],
                    recv_sem=x_rs.at[n, d],
                    device_id=chip(d),
                    device_id_type=MESH,
                )
                copy.start()
                x_copies.append(copy)

        sib_copies, x_copies = [], []
        for n in range(N_RS):
            part[n] = jnp.dot(lhs, weight[:, n * RS_W : (n + 1) * RS_W], preferred_element_type=F32)
            sib_out[n] = part[n, pl.ds(other_half, 64), :].astype(BF16)
            copy = pltpu.make_async_remote_copy(
                src_ref=sib_out.at[n],
                dst_ref=sib_in.at[n],
                send_sem=sib_ss.at[n],
                recv_sem=sib_rs.at[n],
                device_id=sibling,
                device_id_type=MESH,
            )
            copy.start()
            sib_copies.append(copy)
            if n > 0:
                chips(n - 1)
        chips(N_RS - 1)

        def own(n):
            total = part[n, pl.ds(my_rows, OWN), :]
            for i, d in enumerate((2, 1, 3)):
                x_copies[3 * n + i].wait_recv()
                total = total + x_in[n, d].astype(F32)
            return total

        def finish():
            for copy in sib_copies + x_copies:
                copy.wait_send()

        return own, finish

    def normalize(square_sum, gain):
        scale = lax.rsqrt(square_sum / D + EPSILON)
        for n in range(N_RS):
            cols = slice(n * RS_W, (n + 1) * RS_W)
            nrm[pl.ds(my_rows, OWN), cols] = (res[:, cols] * scale * gain[:, cols]).astype(BF16)

    def share_rows():
        ag = {}

        def copy_rows(k, row, send, recv, who):
            ref = nrm.at[pl.ds(pl.multiple_of(row, OWN), OWN), pl.ds(k * AG_W, AG_W)]
            return pltpu.make_async_remote_copy(
                src_ref=ref, dst_ref=ref, send_sem=send, recv_sem=recv, device_id=who, device_id_type=MESH
            )

        for k in range(N_AG):
            for d in (2, 1, 3):
                ag[k, d] = copy_rows(k, my_rows, agx_s.at[k, d], agx_r.at[k, d], chip(d))
                ag[k, d].start()
            ag[k, 4] = copy_rows(k, my_rows, ags_s.at[k, 0], ags_r.at[k, 0], sibling)
            ag[k, 4].start()

        def ready(k):
            for d in (1, 3, 2):
                row = 64 * c + OWN * add4(x, -d)
                copy_rows(k, row, agx_s.at[k, d], agx_r.at[k, d], sibling).wait_recv()
                ag[k, 4 + d] = copy_rows(k, row, ags_s.at[k, d], ags_r.at[k, d], sibling)
                ag[k, 4 + d].start()
            for d in (0, 1, 3, 2):
                row = 64 * (1 - c) + OWN * add4(x, -d)
                copy_rows(k, row, ags_s.at[k, d], ags_r.at[k, d], sibling).wait_recv()

        def finish():
            for copy in ag.values():
                copy.wait_send()

        return ready, finish

    def after_attention(own, gain):
        square_sum = jnp.zeros((OWN, 1), F32)
        for n in range(N_RS):
            cols = slice(n * RS_W, (n + 1) * RS_W)
            total = (res[:, cols] + own(n)).astype(BF16).astype(F32)
            res[:, cols] = total
            square_sum += jnp.sum(total * total, axis=-1, keepdims=True)
        normalize(square_sum, gain)

    def between_passes(own):
        take = accepted[:, :1] == 1
        square_sum = jnp.zeros((OWN, 1), F32)
        for n in range(N_RS):
            cols = slice(n * RS_W, (n + 1) * RS_W)
            first = (res[:, cols] + own(n)).astype(BF16).astype(F32)
            total = jnp.where(take, tok_v[:, cols].astype(F32), first)
            res[:, cols] = total
            square_sum += jnp.sum(total * total, axis=-1, keepdims=True)
        normalize(square_sum, attn_gain)

    def activate():
        gate = g_acc[...]
        hid[...] = (gate / (1.0 + jnp.exp(-gate)) * u_acc[...]).astype(BF16)

    def gate_up_item(mat, a, b, fresh=False):
        acc = (g_acc, u_acc)[mat]
        at = pl.ds(pl.multiple_of(index(mat, a, b) * SHARD, SHARD), SHARD)
        product = jnp.dot(nrm[:, at], full[mat][at, :], preferred_element_type=F32)
        if fresh:
            acc[...] = product
        else:
            acc[...] += product

    def attended():
        return att[...].reshape(ROWS, HEADS * HEAD_DIM)

    gather_0()
    loads["blocks"].wait()
    norm_local()
    res[...] = x_v[pl.ds(my_rows, OWN), :].astype(F32)
    loads["wq"].wait()
    loads["wkv"].wait()
    project(lambda k: None)
    gather_1()
    loads["prompt"].wait()
    loads["cache"].wait()
    attention()
    loads["wo"].wait()
    own, rs_done = reduce_scatter(attended(), wo_v)
    forward(0)
    after_attention(own, mlp_gain)
    rs_done()
    ready, ag_done = share_rows()
    gather_3()
    for k in range(N_AG):
        ready(k)
    ag_done()
    for a in (0, -1, 1, 2):
        for mat in (0, 1):
            gate_up_item(mat, a, 0, fresh=a == 0)
    for b in (-1, 1):
        for mat in (0, 1):
            gate_up_item(mat, 0, b)
    for a in (-1, 1, 2):
        forward(a)
        for b in (-1, 1):
            for mat in (0, 1):
                gate_up_item(mat, a, b)
    for a in (0, -1, 1, 2):
        for mat in (0, 1):
            g_wait(mat, a, 2, 0)
            g_wait(mat, a, 2, 1)
            gate_up_item(mat, a, 2)
    for copy in sends[0] + sends[1]:
        copy.wait_send()
    activate()
    loads["wd"].wait()
    loads["tok"].wait()
    own, rs_done = reduce_scatter(hid[...], wd_v)
    between_passes(own)
    rs_done()

    ready, ag_done = share_rows()
    project(ready)
    ag_done()
    attention()
    own, rs_done = reduce_scatter(attended(), wo_v)
    after_attention(own, mlp_gain)
    rs_done()
    ready, ag_done = share_rows()
    for k in range(N_AG):
        ready(k)
        for part_k in range(2):
            start = k * AG_W + part_k * (AG_W // 2)
            at = slice(start, start + AG_W // 2)
            for acc, weight in ((g_acc, gate_v), (u_acc, up_v)):
                product = jnp.dot(nrm[:, at], weight[at, :], preferred_element_type=F32)
                if start == 0:
                    acc[...] = product
                else:
                    acc[...] += product
    ag_done()
    activate()
    own, rs_done = reduce_scatter(hid[...], wd_v)
    for n in range(N_RS):
        cols = slice(n * RS_W, (n + 1) * RS_W)
        nrm[pl.ds(my_rows, OWN), cols] = (res[:, cols] + own(n)).astype(BF16)
    rs_done()
    ready, ag_done = share_rows()
    for k in range(N_AG):
        ready(k)
    ag_done()
    copy = pltpu.make_async_copy(nrm, out, load_sem.at[0])
    copy.start()
    copy.wait()


def body(
    blocks, token_embed, accepted, prompt_len, cache_len, prompt_kv, cache_kv, attn_gain,
    w_q, w_kv, w_o, mlp_gain, w_gate, w_up, w_down,
):
    prompt_size = prompt_len[0]
    cache_sizes = cache_len[0]
    positions = (
        prompt_size + cache_sizes[:, None] + jnp.arange(BLOCK, dtype=jnp.int32)[None, :]
    ).reshape(-1)
    half = HEAD_DIM // 2
    frequency = THETA ** (-2.0 * jnp.arange(half, dtype=F32) / HEAD_DIM)
    angles = positions.astype(F32)[:, None] * frequency[None, :]
    cosine, sine = jnp.cos(angles), jnp.sin(angles)
    cos = jnp.concatenate([cosine, cosine], axis=-1)
    sin = jnp.concatenate([-sine, sine], axis=-1)
    m = lax.axis_index("mlp")
    start = 64 * (m % 2) + OWN * (m // 2)
    taken = jnp.broadcast_to(lax.dynamic_slice(accepted, (start,), (OWN,))[:, None], (OWN, 128))
    lens = jnp.concatenate([prompt_len, cache_sizes])

    vmem = pl.BlockSpec(memory_space=pltpu.VMEM)
    anywhere = pl.BlockSpec(memory_space=pl.ANY)
    dma = pltpu.SemaphoreType.DMA
    return pl.pallas_call(
        kernel,
        out_shape=jax.ShapeDtypeStruct((ROWS, D), BF16),
        in_specs=[pl.BlockSpec(memory_space=pltpu.SMEM)] + [vmem] * 5 + [anywhere] * 10,
        out_specs=anywhere,
        scratch_shapes=[
            pltpu.VMEM((ROWS, D), BF16),
            pltpu.VMEM((OWN, D), BF16),
            pltpu.VMEM((PMAX, 2 * HEAD_DIM), BF16),
            pltpu.VMEM((REQS, CACHE, 2 * HEAD_DIM), BF16),
            pltpu.VMEM((D, HEADS * HEAD_DIM), BF16),
            pltpu.VMEM((D, 2 * HEAD_DIM), BF16),
            pltpu.VMEM((HEADS * HEAD_DIM, D), BF16),
            pltpu.VMEM((D, HIDDEN), BF16),
            pltpu.VMEM((D, HIDDEN), BF16),
            pltpu.VMEM((HIDDEN, D), BF16),
            pltpu.VMEM((ROWS, D), BF16),
            pltpu.VMEM((ROWS, (HEADS + 2) * HEAD_DIM), F32),
            pltpu.VMEM((REQS, HEADS * BLOCK, HEAD_DIM), BF16),
            pltpu.VMEM((REQS, BLOCK, HEAD_DIM), BF16),
            pltpu.VMEM((REQS, BLOCK, HEAD_DIM), BF16),
            pltpu.VMEM((REQS, BLOCK, HEADS * HEAD_DIM), BF16),
            pltpu.VMEM((ROWS, HIDDEN), F32),
            pltpu.VMEM((ROWS, HIDDEN), F32),
            pltpu.VMEM((ROWS, HIDDEN), BF16),
            pltpu.VMEM((N_RS, ROWS, RS_W), F32),
            pltpu.VMEM((N_RS, 64, RS_W), BF16),
            pltpu.VMEM((N_RS, 64, RS_W), BF16),
            pltpu.VMEM((N_RS, 4, OWN, RS_W), BF16),
            pltpu.VMEM((N_RS, 4, OWN, RS_W), BF16),
            pltpu.VMEM((OWN, D), F32),
            dma((10,)),
            dma((2, 20)),
            dma((2, 4, 4, 2)),
            dma((N_RS,)),
            dma((N_RS,)),
            dma((N_RS, 4)),
            dma((N_RS, 4)),
            dma((N_AG, 4)),
            dma((N_AG, 4)),
            dma((N_AG, 4)),
            dma((N_AG, 4)),
        ],
        compiler_params=pltpu.CompilerParams(
            collective_id=0, has_side_effects=True, vmem_limit_bytes=60 * 2**20
        ),
        name="two_passes",
    )(
        lens, cos, sin, taken, attn_gain[None, :], mlp_gain[None, :],
        blocks, token_embed, prompt_kv[0], cache_kv[0], w_q, w_kv, w_o, w_gate, w_up, w_down,
    )


def solution(mesh):
    return jax.shard_map(
        body,
        mesh=mesh,
        in_specs=(
            P("req", None),
            P("req", None),
            P("req"),
            P("req"),
            P("req", None),
            P("req", None, "mlp"),
            P("req", None, None, "mlp"),
            P(),
            P(None, "mlp"),
            P(None, "mlp"),
            P("mlp", None),
            P(),
            P("req", "mlp"),
            P("req", "mlp"),
            P("mlp", None),
        ),
        out_specs=P("req", None),
        check_vma=False,
    )
```

time: 507 us -> 159 us (0.31)
  waiting for transfers between devices: 325 us -> 0 us
  Pallas kernels: 0 us -> 152 us
  matrix products: 72.5 us -> 0 us
  local copies, waits for them, and re-layouts: 45.8 us -> 3.77 us
  other arithmetic: 43.5 us -> 3.06 us
  between operations: 15.6 us -> 0.67 us
    psum x4 -> x0, waiting for transfers between devices: 260 us -> none  [the longest x2 132 us: one_pass(): lax.psum(jnp.dot(attended, w_o, preferred_element_type=jnp.float32), 'mlp')]
    pallas_call x0 -> x1, Pallas kernels: none -> 152 us  [body(): pl.pallas_call(kernel, out_shape=jax.ShapeDtypeStruct((ROWS, D), BF16), i...]
    dot_general x106 -> x0, matrix products: 72.5 us -> none  [the longest x2 18 us: one_pass(): jnp.dot(hidden, w_down, preferred_element_type=jnp.float32)]
    all_gather x2 -> x0, waiting for transfers between devices: 63.9 us -> none  [the longest x1 62.8 us: one_pass(): lax.all_gather(w_up, 'req', axis=0, tiled=True)]
    lt x32 -> x0, other arithmetic: 20.9 us -> none  [the longest x16 10.5 us: attend_one(): prompt_ok = jnp.arange(prompt_part.shape[0], dtype=jnp.int32) < prompt_size]
    squeeze x16 -> x0, local copies, waits for them, and re-layouts: 17.3 us -> none  [one_pass(): lax.map(attend_request, (queries.reshape(REQS, BLOCK, local_heads, HEAD_D...]
    reduce_sum x52 -> x0, other arithmetic: 14.8 us -> none  [the longest x4 8.42 us: rms_scale(): mean_square = jnp.mean(widened * widened, axis=-1, keepdims=True)]
    dynamic_slice x16 -> x1, local copies, waits for them, and re-layouts: 10.3 us -> 0.73 us  [body(): lax.dynamic_slice(accepted, (start,), (OWN,))[:, None]]
  transfers between devices with their start and end apart: 6 -> 0, of which waited for: 6 -> 0; matrix products, arithmetic and copies ran while one was open for 2% -> 0% of each run, Pallas kernels for 0% -> 0%
where the time goes in v1:
time: 159 us
  Pallas kernels  152 us (96%)
  local copies, waits for them, and re-layouts  3.77 us (2%)
  other arithmetic  3.06 us (2%)
    pallas_call x1, Pallas kernels, body(): pl.pallas_call(kernel, out_shape=jax.ShapeDtypeStruct((ROWS, D), BF16), i...  152 us

profile of v1, /device:TPU:1, one launch (start us, length us, event | category | flops | bytes accessed | tf_op | source)
XLA Modules:
  0.0 159.0 jit_solution(4415683759597082819)
XLA Ops:
  0.7 0.7 dynamic_slice.3
  1.4 1.3 pad_add_fusion.lens
  2.6 0.7 broadcast_add_fusion
  3.3 0.1 add_convert_fusion
  3.4 0.1 convert_element_type.11
  3.5 0.7 broadcast_in_dim.6.accepted
  4.1 0.3 fusion
  4.5 0.8 pad_maximum_fusion
  5.2 151.5 %two_passes.1 = bf16[128,4096]{1,0:T(8,128)(2,1)} custom-call(s32[9]{0:T(128)} %pad_add_fusion.lens, f32[128,128]{1,0:T(8,128)} %get-tuple-element.8.cos, f32[128,128]{1,0:T(8,128)} %get-tuple-element.9.sin, s32[16,128]{1,0:T(8,128)} %broadcast_in_dim.6.accepted, f32[1,4096]{1,0:T(1,128)} %bitcast.10, f32[1,4096]{1,0:T(1,128)} %bitcast.11, ...), custom_call_target="tpu_custom_call" | custom-call | tf_op jit(solution)/shard_map/two_passes/pallas_call | solution.py:465
  156.7 2.3 %copy.18 = bf16[128,4096]{1,0:T(8,128)(2,1)} copy(bf16[128,4096]{1,0:T(8,128)(2,1)} %two_passes.1) | data formatting | bytes 2097152
  (1 shorter events, 0.0 us)

commit v2 on v1

--- a/solution.py
+++ b/solution.py
@@ -1,4 +1,3 @@
-import functools
 import math
 
 import jax
@@ -7,6 +6,7 @@
 from jax.experimental import pallas as pl
 from jax.experimental.pallas import tpu as pltpu
 from jax.sharding import PartitionSpec as P
+import numpy as np
 
 D = 4096
 HEAD_DIM = 128
@@ -18,6 +18,7 @@
 PMAX = 512
 HIDDEN = 896
 SHARD = 256
+SLICE = 1024
 OWN = 16
 EPSILON = 1e-05
 THETA = 500000.0
@@ -31,13 +32,15 @@
 
 
 def kernel(
-    lens, cos, sin, accepted, attn_gain, mlp_gain,
+    prompt_len, cache_len, accepted, frequency, attn_gain, mlp_gain,
     blocks, token, prompt, cache, w_q, w_kv, w_o, w_gate, w_up, w_down,
     out,
     x_v, tok_v, prm_v, cache_v, wq_v, wkv_v, wo_v, gate_v, up_v, wd_v,
     nrm, qkv, q_s, k_s, v_s, att, g_acc, u_acc, hid,
-    part, sib_out, sib_in, x_out, x_in, res,
+    part, sib_out, sib_in, x_out, x_in, res, cos, sin,
+    rows_k, far_out, far_in, near_out, near_in,
     load_sem, g_send, g_recv, sib_ss, sib_rs, x_ss, x_rs, agx_s, agx_r, ags_s, ags_r,
+    ky_s, ky_r, kx_s, kx_r, ks_s, ks_r, far_s, far_r, near_s, near_r,
 ):
     r = lax.axis_index("req")
     m = lax.axis_index("mlp")
@@ -80,7 +83,7 @@
         loads[name] = copy
 
     barrier = pltpu.get_barrier_semaphore()
-    partners = [chip(1), chip(2), chip(3), sibling, plane(0, 1), plane(0, 3), plane(1, 0), plane(3, 0)]
+    partners = [chip(1), chip(2), chip(3), sibling, plane(0, 1), plane(0, 3), plane(1, 0), plane(3, 0), plane(2, 0)]
     for who in partners:
         pl.semaphore_signal(barrier, inc=1, device_id=who, device_id_type=MESH)
     pl.semaphore_wait(barrier, len(partners))
@@ -135,30 +138,35 @@
                 g_start(mat, 0, 0, None, axis, 1)
                 g_start(mat, 0, 0, None, axis, -1)
 
-    def gather_1():
-        for mat in (0, 1):
-            g_wait(mat, -1, 0)
-            g_start(mat, -1, 0, 0, 0, 1)
-            g_wait(mat, 1, 0)
-            g_start(mat, 1, 0, 1, 0, -1)
-        for a in (-1, 1):
-            for mat in (0, 1):
-                g_start(mat, a, 0, None, 1, 1)
-                g_start(mat, a, 0, None, 1, -1)
-
-    def forward(a):
-        for mat in (0, 1):
-            g_wait(mat, a, -1)
-            g_start(mat, a, -1, 0, 1, 1)
-            g_wait(mat, a, 1)
-            g_start(mat, a, 1, 1, 1, -1)
-
-    def gather_3():
-        for mat in (0, 1):
-            g_wait(mat, 2, 0, 0)
-            g_wait(mat, 2, 0, 1)
-            g_start(mat, 2, 0, None, 1, 1)
-            g_start(mat, 2, 0, None, 1, -1)
+    def turn(mat, axis):
+        for step, half in ((1, 0), (-1, 1)):
+            at = (-step, 0) if axis == 0 else (0, -step)
+            g_wait(mat, *at)
+            g_start(mat, *at, half, axis, step)
+
+    def spread(mat, a):
+        g_start(mat, a, 0, None, 1, 1)
+        g_start(mat, a, 0, None, 1, -1)
+
+    def halves(mat, a, b):
+        g_wait(mat, a, b, 0)
+        g_wait(mat, a, b, 1)
+
+    def forward(mat, a):
+        g_wait(mat, a, -1)
+        g_start(mat, a, -1, 0, 1, 1)
+        g_wait(mat, a, 1)
+        g_start(mat, a, 1, 1, 1, -1)
+
+    def tables():
+        lane = lax.broadcasted_iota(jnp.int32, (BLOCK, HEAD_DIM), 1)
+        row = lax.broadcasted_iota(jnp.int32, (BLOCK, HEAD_DIM), 0)
+        for j in range(REQS):
+            position = row + (prompt_len[0] + cache_len[0, j])
+            angle = position.astype(F32) * frequency[...]
+            cos[BLOCK * j : BLOCK * (j + 1), :] = jnp.cos(angle)
+            sine = jnp.sin(angle)
+            sin[BLOCK * j : BLOCK * (j + 1), :] = jnp.where(lane < HEAD_DIM // 2, -sine, sine)
 
     def norm_local():
         def step(i, carry):
@@ -209,8 +217,8 @@
             s_b = scores(k_s[j])
             at_c = lax.broadcasted_iota(jnp.int32, s_c.shape, 1)
             at_p = lax.broadcasted_iota(jnp.int32, s_p.shape, 1)
-            s_c = jnp.where(at_c < lens[1 + j], s_c, -1e30)
-            s_p = jnp.where(at_p < lens[0], s_p, -1e30)
+            s_c = jnp.where(at_c < cache_len[0, j], s_c, -1e30)
+            s_p = jnp.where(at_p < prompt_len[0], s_p, -1e30)
             top = jnp.maximum(
                 jnp.maximum(jnp.max(s_c, -1, keepdims=True), jnp.max(s_p, -1, keepdims=True)),
                 jnp.max(s_b, -1, keepdims=True),
@@ -332,7 +340,10 @@
         normalize(square_sum, gain)
 
     def between_passes(own):
-        take = accepted[:, :1] == 1
+        lane = lax.broadcasted_iota(jnp.int32, (OWN, ROWS), 1)
+        row = lax.broadcasted_iota(jnp.int32, (OWN, ROWS), 0) + my_rows
+        mine = jnp.where(lane == row, accepted[...].astype(F32), 0.0)
+        take = jnp.sum(mine, axis=-1, keepdims=True) == 1.0
         square_sum = jnp.zeros((OWN, 1), F32)
         for n in range(N_RS):
             cols = slice(n * RS_W, (n + 1) * RS_W)
@@ -346,57 +357,145 @@
         gate = g_acc[...]
         hid[...] = (gate / (1.0 + jnp.exp(-gate)) * u_acc[...]).astype(BF16)
 
-    def gate_up_item(mat, a, b, fresh=False):
-        acc = (g_acc, u_acc)[mat]
-        at = pl.ds(pl.multiple_of(index(mat, a, b) * SHARD, SHARD), SHARD)
-        product = jnp.dot(nrm[:, at], full[mat][at, :], preferred_element_type=F32)
-        if fresh:
-            acc[...] = product
-        else:
-            acc[...] += product
+    def slice_rows():
+        made = {}
+
+        def go(key, src, dst, send, recv, who):
+            made[key] = pltpu.make_async_remote_copy(
+                src_ref=src, dst_ref=dst, send_sem=send, recv_sem=recv, device_id=who, device_id_type=MESH
+            )
+            made[key].start()
+
+        def rows_of(k, core, d):
+            row = 64 * core + OWN * add4(x, d)
+            return rows_k.at[k, pl.ds(pl.multiple_of(row, OWN), OWN)]
+
+        def chunk(dy):
+            return pl.ds(pl.multiple_of(add4(y, dy) * SLICE, SLICE), SLICE)
+
+        def over_x(k):
+            for d in (2, 1, 3):
+                go(("x", k, d), rows_of(k, c, 0), rows_of(k, c, 0), kx_s.at[k, d], kx_r.at[k, d], chip(d))
+            go(("s", k, 0), rows_of(k, c, 0), rows_of(k, c, 0), ks_s.at[k, 0], ks_r.at[k, 0], sibling)
+
+        for dy in (2, 1, 3):
+            k = (-dy) % 4
+            src = nrm.at[pl.ds(my_rows, OWN), chunk(dy)]
+            go(("y", k), src, rows_of(k, c, 0), ky_s.at[k], ky_r.at[k], plane(dy, 0))
+        rows_k[0, pl.ds(my_rows, OWN), :] = nrm[pl.ds(my_rows, OWN), chunk(0)]
+        over_x(0)
+        for k in (2, 1, 3):
+            made["y", k].wait_recv()
+            over_x(k)
+
+        def ready(k):
+            for d in (1, 3, 2):
+                made["x", k, d].wait_recv()
+                ref = rows_of(k, c, -d)
+                go(("s", k, d), ref, ref, ks_s.at[k, d], ks_r.at[k, d], sibling)
+            for d in (0, 1, 3, 2):
+                made["s", k, d].wait_recv()
+
+        def finish():
+            for copy in made.values():
+                copy.wait_send()
+
+        return ready, finish
+
+    def slice_gate_up(ready):
+        made = []
+        at = pl.ds(pl.multiple_of(y * SLICE, SLICE), SLICE)
+
+        def product(k, mat):
+            return jnp.dot(rows_k[k], full[mat][at, :], preferred_element_type=F32)
+
+        def go(src, dst, send, recv, dy):
+            copy = pltpu.make_async_remote_copy(
+                src_ref=src, dst_ref=dst, send_sem=send, recv_sem=recv,
+                device_id=plane(dy, 0), device_id_type=MESH,
+            )
+            copy.start()
+            made.append(copy)
+            return copy
+
+        ready(2)
+        far = []
+        for mat in (0, 1):
+            far_out[mat] = product(2, mat).astype(BF16)
+            far.append(
+                go(far_out.at[mat], far_in.at[mat], far_s.at[mat], far_r.at[mat], 1 - 2 * mat)
+            )
+        near = []
+
+        def send_near(i, mat, value):
+            near_out[i, mat] = value.astype(BF16)
+            near.append(
+                go(
+                    near_out.at[i, mat], near_in.at[i, mat],
+                    near_s.at[i, mat], near_r.at[i, mat], 1 - 2 * i,
+                )
+            )
+
+        ready(1)
+        send_near(0, 1, product(1, 1))
+        ready(3)
+        send_near(1, 0, product(3, 0))
+        value = product(1, 0)
+        far[0].wait_recv()
+        send_near(0, 0, value + far_in[0].astype(F32))
+        value = product(3, 1)
+        far[1].wait_recv()
+        send_near(1, 1, value + far_in[1].astype(F32))
+        ready(0)
+        for mat, acc in ((0, g_acc), (1, u_acc)):
+            acc[...] = product(0, mat)
+
+        def collect():
+            for copy in near:
+                copy.wait_recv()
+            for mat, acc in ((0, g_acc), (1, u_acc)):
+                acc[...] += near_in[0, mat].astype(F32) + near_in[1, mat].astype(F32)
+
+        def finish():
+            for copy in made:
+                copy.wait_send()
+
+        return collect, finish
 
     def attended():
         return att[...].reshape(ROWS, HEADS * HEAD_DIM)
 
     gather_0()
+    tables()
     loads["blocks"].wait()
     norm_local()
     res[...] = x_v[pl.ds(my_rows, OWN), :].astype(F32)
     loads["wq"].wait()
     loads["wkv"].wait()
     project(lambda k: None)
-    gather_1()
     loads["prompt"].wait()
     loads["cache"].wait()
     attention()
     loads["wo"].wait()
     own, rs_done = reduce_scatter(attended(), wo_v)
-    forward(0)
+    turn(0, 0)
+    turn(1, 1)
+    turn(1, 0)
+    turn(0, 1)
     after_attention(own, mlp_gain)
     rs_done()
-    ready, ag_done = share_rows()
-    gather_3()
-    for k in range(N_AG):
-        ready(k)
-    ag_done()
-    for a in (0, -1, 1, 2):
-        for mat in (0, 1):
-            gate_up_item(mat, a, 0, fresh=a == 0)
-    for b in (-1, 1):
-        for mat in (0, 1):
-            gate_up_item(mat, 0, b)
+    ready, rows_done = slice_rows()
+    halves(0, 2, 0)
+    halves(1, 0, 2)
+    collect, sums_done = slice_gate_up(ready)
+    halves(1, 2, 0)
     for a in (-1, 1, 2):
-        forward(a)
-        for b in (-1, 1):
-            for mat in (0, 1):
-                gate_up_item(mat, a, b)
-    for a in (0, -1, 1, 2):
-        for mat in (0, 1):
-            g_wait(mat, a, 2, 0)
-            g_wait(mat, a, 2, 1)
-            gate_up_item(mat, a, 2)
-    for copy in sends[0] + sends[1]:
-        copy.wait_send()
+        spread(1, a)
+    collect()
+    for a in (-1, 1, 2):
+        spread(0, a)
+    rows_done()
+    sums_done()
     activate()
     loads["wd"].wait()
     loads["tok"].wait()
@@ -407,11 +506,20 @@
     ready, ag_done = share_rows()
     project(ready)
     ag_done()
+    for a in (-1, 1, 2):
+        forward(1, a)
     attention()
     own, rs_done = reduce_scatter(attended(), wo_v)
+    for a in (-1, 1):
+        forward(0, a)
     after_attention(own, mlp_gain)
     rs_done()
     ready, ag_done = share_rows()
+    forward(0, 2)
+    halves(0, 0, 2)
+    for a in (-1, 1, 2):
+        halves(0, a, 2)
+        halves(1, a, 2)
     for k in range(N_AG):
         ready(k)
         for part_k in range(2):
@@ -424,6 +532,8 @@
                 else:
                     acc[...] += product
     ag_done()
+    for copy in sends[0] + sends[1]:
+        copy.wait_send()
     activate()
     own, rs_done = reduce_scatter(hid[...], wd_v)
     for n in range(N_RS):
@@ -443,21 +553,9 @@
     blocks, token_embed, accepted, prompt_len, cache_len, prompt_kv, cache_kv, attn_gain,
     w_q, w_kv, w_o, mlp_gain, w_gate, w_up, w_down,
 ):
-    prompt_size = prompt_len[0]
-    cache_sizes = cache_len[0]
-    positions = (
-        prompt_size + cache_sizes[:, None] + jnp.arange(BLOCK, dtype=jnp.int32)[None, :]
-    ).reshape(-1)
-    half = HEAD_DIM // 2
-    frequency = THETA ** (-2.0 * jnp.arange(half, dtype=F32) / HEAD_DIM)
-    angles = positions.astype(F32)[:, None] * frequency[None, :]
-    cosine, sine = jnp.cos(angles), jnp.sin(angles)
-    cos = jnp.concatenate([cosine, cosine], axis=-1)
-    sin = jnp.concatenate([-sine, sine], axis=-1)
-    m = lax.axis_index("mlp")
-    start = 64 * (m % 2) + OWN * (m // 2)
-    taken = jnp.broadcast_to(lax.dynamic_slice(accepted, (start,), (OWN,))[:, None], (OWN, 128))
-    lens = jnp.concatenate([prompt_len, cache_sizes])
+    half = np.arange(HEAD_DIM // 2, dtype=np.float32)
+    frequency = np.float32(THETA) ** (np.float32(-2.0) * half / np.float32(HEAD_DIM))
+    frequency = jnp.asarray(np.concatenate([frequency, frequency])[None, :], dtype=F32)
 
     vmem = pl.BlockSpec(memory_space=pltpu.VMEM)
     anywhere = pl.BlockSpec(memory_space=pl.ANY)
@@ -465,7 +563,7 @@
     return pl.pallas_call(
         kernel,
         out_shape=jax.ShapeDtypeStruct((ROWS, D), BF16),
-        in_specs=[pl.BlockSpec(memory_space=pltpu.SMEM)] + [vmem] * 5 + [anywhere] * 10,
+        in_specs=[pl.BlockSpec(memory_space=pltpu.SMEM)] * 2 + [vmem] * 4 + [anywhere] * 10,
         out_specs=anywhere,
         scratch_shapes=[
             pltpu.VMEM((ROWS, D), BF16),
@@ -493,6 +591,13 @@
             pltpu.VMEM((N_RS, 4, OWN, RS_W), BF16),
             pltpu.VMEM((N_RS, 4, OWN, RS_W), BF16),
             pltpu.VMEM((OWN, D), F32),
+            pltpu.VMEM((ROWS, HEAD_DIM), F32),
+            pltpu.VMEM((ROWS, HEAD_DIM), F32),
+            pltpu.VMEM((4, ROWS, SLICE), BF16),
+            pltpu.VMEM((2, ROWS, HIDDEN), BF16),
+            pltpu.VMEM((2, ROWS, HIDDEN), BF16),
+            pltpu.VMEM((2, 2, ROWS, HIDDEN), BF16),
+            pltpu.VMEM((2, 2, ROWS, HIDDEN), BF16),
             dma((10,)),
             dma((2, 20)),
             dma((2, 4, 4, 2)),
@@ -504,13 +609,23 @@
             dma((N_AG, 4)),
             dma((N_AG, 4)),
             dma((N_AG, 4)),
+            dma((4,)),
+            dma((4,)),
+            dma((4, 4)),
+            dma((4, 4)),
+            dma((4, 4)),
+            dma((4, 4)),
+            dma((2,)),
+            dma((2,)),
+            dma((2, 2)),
+            dma((2, 2)),
         ],
         compiler_params=pltpu.CompilerParams(
             collective_id=0, has_side_effects=True, vmem_limit_bytes=60 * 2**20
         ),
         name="two_passes",
     )(
-        lens, cos, sin, taken, attn_gain[None, :], mlp_gain[None, :],
+        prompt_len, cache_len, accepted[None, :], frequency, attn_gain[None, :], mlp_gain[None, :],
         blocks, token_embed, prompt_kv[0], cache_kv[0], w_q, w_kv, w_o, w_gate, w_up, w_down,
     )
 

time: 159 us -> 146 us (0.918)
  Pallas kernels: 152 us -> 143 us
  other arithmetic: 3.06 us -> 0 us
    pallas_call x1, Pallas kernels: 152 us -> 143 us  [body(): pl.pallas_call(kernel, out_shape=jax.ShapeDtypeStruct((ROWS, D), BF16), i...]
    concatenate x2 -> x0, other arithmetic: 2.02 us -> none  [the longest x1 1.26 us: body(): lens = jnp.concatenate([prompt_len, cache_sizes])]
where the time goes in v2:
time: 146 us
  Pallas kernels  143 us (98%)
  local copies, waits for them, and re-layouts  2.29 us (2%)
    pallas_call x1, Pallas kernels, body(): pl.pallas_call(kernel, out_shape=jax.ShapeDtypeStruct((ROWS, D), BF16), i...  143 us

profile of v2, /device:TPU:1, one launch (start us, length us, event | category | flops | bytes accessed | tf_op | source)
XLA Modules:
  0.0 146.2 jit_solution(12419414695361097081)
XLA Ops:
  0.7 143.3 %two_passes.1 = bf16[128,4096]{1,0:T(8,128)(2,1)} custom-call(s32[1]{0:T(128)S(6)} %copy.18.prompt_len, s32[1,8]{1,0:T(1,128)} %cache_len.1, s32[1,128]{1,0:T(1,128)} %bitcast.9, f32[1,128]{1,0:T(1,128)} %constant.2.clone.frequency, f32[1,4096]{1,0:T(1,128)} %bitcast.7, f32[1,4096]{1,0:T(1,128)} %bitcast.8, bf16[128,4096]{1,0:T(8,128)(2,1)} %blocks.1, ...), custom_call_target="tpu_custom_call" | custom-call | tf_op jit(solution)/shard_map/two_passes/pallas_call | solution.py:563
  144.0 2.3 %copy.19 = bf16[128,4096]{1,0:T(8,128)(2,1)} copy(bf16[128,4096]{1,0:T(8,128)(2,1)} %two_passes.1) | data formatting | bytes 2097152

commit v3 on v2

--- a/solution.py
+++ b/solution.py
@@ -178,32 +178,27 @@
 
         lax.fori_loop(0, ROWS // OWN, step, 0)
 
-    def project(ready):
-        for k in range(N_AG):
-            ready(k)
-            cols = slice(k * AG_W, (k + 1) * AG_W)
-            lhs = nrm[:, cols]
-            q_part = jnp.dot(lhs, wq_v[cols, :], preferred_element_type=F32)
-            kv_part = jnp.dot(lhs, wkv_v[cols, :], preferred_element_type=F32)
-            if k == 0:
-                qkv[:, : HEADS * HEAD_DIM] = q_part
-                qkv[:, HEADS * HEAD_DIM :] = kv_part
-            else:
-                qkv[:, : HEADS * HEAD_DIM] += q_part
-                qkv[:, HEADS * HEAD_DIM :] += kv_part
-
-    def attention():
+    def project(lo, hi):
+        lhs = nrm[lo:hi, :]
+        qkv[lo:hi, : HEADS * HEAD_DIM] = jnp.dot(lhs, wq_v[...], preferred_element_type=F32)
+        qkv[lo:hi, HEADS * HEAD_DIM :] = jnp.dot(lhs, wkv_v[...], preferred_element_type=F32)
+
+    def attention(lo, hi):
+        first, last = lo // BLOCK, hi // BLOCK
+        count = last - first
+
         def rope(values):
-            return (values * cos[...] + pltpu.roll(values, HEAD_DIM // 2, 1) * sin[...]).astype(BF16)
+            turned = values * cos[lo:hi, :] + pltpu.roll(values, HEAD_DIM // 2, 1) * sin[lo:hi, :]
+            return turned.astype(BF16).reshape(count, BLOCK, HEAD_DIM)
 
         for h in range(HEADS):
-            q_s[:, BLOCK * h : BLOCK * (h + 1), :] = rope(
-                qkv[:, HEAD_DIM * h : HEAD_DIM * (h + 1)]
-            ).reshape(REQS, BLOCK, HEAD_DIM)
+            q_s[first:last, BLOCK * h : BLOCK * (h + 1), :] = rope(
+                qkv[lo:hi, HEAD_DIM * h : HEAD_DIM * (h + 1)]
+            )
         base = HEADS * HEAD_DIM
-        k_s[...] = rope(qkv[:, base : base + HEAD_DIM]).reshape(REQS, BLOCK, HEAD_DIM)
-        v_s[...] = qkv[:, base + HEAD_DIM :].astype(BF16).reshape(REQS, BLOCK, HEAD_DIM)
-        scale = 1.0 / math.sqrt(HEAD_DIM)
+        k_s[first:last] = rope(qkv[lo:hi, base : base + HEAD_DIM])
+        v_s[first:last] = qkv[lo:hi, base + HEAD_DIM :].astype(BF16).reshape(count, BLOCK, HEAD_DIM)
+        scale = math.log2(math.e) / math.sqrt(HEAD_DIM)
         contract = (((1,), (1,)), ((), ()))
 
         def step(j, carry):
@@ -223,9 +218,9 @@
                 jnp.maximum(jnp.max(s_c, -1, keepdims=True), jnp.max(s_p, -1, keepdims=True)),
                 jnp.max(s_b, -1, keepdims=True),
             )
-            e_c = jnp.exp(s_c - top)
-            e_p = jnp.exp(s_p - top)
-            e_b = jnp.exp(s_b - top)
+            e_c = jnp.exp2(s_c - top)
+            e_p = jnp.exp2(s_p - top)
+            e_b = jnp.exp2(s_b - top)
             total = (
                 jnp.sum(e_c, -1, keepdims=True)
                 + jnp.sum(e_p, -1, keepdims=True)
@@ -239,7 +234,7 @@
                 att[j, :, HEAD_DIM * h : HEAD_DIM * (h + 1)] = mixed[BLOCK * h : BLOCK * (h + 1)]
             return carry
 
-        lax.fori_loop(0, REQS, step, 0)
+        lax.fori_loop(first, last, step, 0, unroll=2)
 
     pending = []
 
@@ -298,38 +293,6 @@
             cols = slice(n * RS_W, (n + 1) * RS_W)
             nrm[pl.ds(my_rows, OWN), cols] = (res[:, cols] * scale * gain[:, cols]).astype(BF16)
 
-    def share_rows():
-        ag = {}
-
-        def copy_rows(k, row, send, recv, who):
-            ref = nrm.at[pl.ds(pl.multiple_of(row, OWN), OWN), pl.ds(k * AG_W, AG_W)]
-            return pltpu.make_async_remote_copy(
-                src_ref=ref, dst_ref=ref, send_sem=send, recv_sem=recv, device_id=who, device_id_type=MESH
-            )
-
-        for k in range(N_AG):
-            for d in (2, 1, 3):
-                ag[k, d] = copy_rows(k, my_rows, agx_s.at[k, d], agx_r.at[k, d], chip(d))
-                ag[k, d].start()
-            ag[k, 4] = copy_rows(k, my_rows, ags_s.at[k, 0], ags_r.at[k, 0], sibling)
-            ag[k, 4].start()
-
-        def ready(k):
-            for d in (1, 3, 2):
-                row = 64 * c + OWN * add4(x, -d)
-                copy_rows(k, row, agx_s.at[k, d], agx_r.at[k, d], sibling).wait_recv()
-                ag[k, 4 + d] = copy_rows(k, row, ags_s.at[k, d], ags_r.at[k, d], sibling)
-                ag[k, 4 + d].start()
-            for d in (0, 1, 3, 2):
-                row = 64 * (1 - c) + OWN * add4(x, -d)
-                copy_rows(k, row, ags_s.at[k, d], ags_r.at[k, d], sibling).wait_recv()
-
-        def finish():
-            for copy in ag.values():
-                copy.wait_send()
-
-        return ready, finish
-
     def after_attention(own, gain):
         square_sum = jnp.zeros((OWN, 1), F32)
         for n in range(N_RS):
@@ -353,9 +316,15 @@
             square_sum += jnp.sum(total * total, axis=-1, keepdims=True)
         normalize(square_sum, attn_gain)
 
-    def activate():
-        gate = g_acc[...]
-        hid[...] = (gate / (1.0 + jnp.exp(-gate)) * u_acc[...]).astype(BF16)
+    def activate(lo, hi):
+        gate = g_acc[lo:hi, :]
+        hid[lo:hi, :] = (gate / (1.0 + jnp.exp(-gate)) * u_acc[lo:hi, :]).astype(BF16)
+
+    def gate_up(lo, hi):
+        lhs = nrm[lo:hi, :]
+        g_acc[lo:hi, :] = jnp.dot(lhs, gate_v[...], preferred_element_type=F32)
+        u_acc[lo:hi, :] = jnp.dot(lhs, up_v[...], preferred_element_type=F32)
+        activate(lo, hi)
 
     def slice_rows():
         made = {}
@@ -462,8 +431,129 @@
 
         return collect, finish
 
-    def attended():
-        return att[...].reshape(ROWS, HEADS * HEAD_DIM)
+    def attended(lo, hi):
+        return att[lo // BLOCK : hi // BLOCK].reshape(hi - lo, HEADS * HEAD_DIM)
+
+    def half_scatter(h, lhs, weight):
+        rows = slice(64 * h, 64 * (h + 1))
+
+        def to_sibling(n):
+            return pltpu.make_async_remote_copy(
+                src_ref=sib_out.at[n],
+                dst_ref=sib_in.at[n],
+                send_sem=sib_ss.at[n],
+                recv_sem=sib_rs.at[n],
+                device_id=sibling,
+                device_id_type=MESH,
+            )
+
+        def to_chip(n, d):
+            return pltpu.make_async_remote_copy(
+                src_ref=x_out.at[n, add4(x, d)],
+                dst_ref=x_in.at[n, d],
+                send_sem=x_ss.at[n, d],
+                recv_sem=x_rs.at[n, d],
+                device_id=chip(d),
+                device_id_type=MESH,
+            )
+
+        def chips(n):
+            @pl.when(c == h)
+            def _():
+                to_sibling(n).wait_recv()
+                total = part[n, rows, :] + sib_in[n].astype(F32)
+                part[n, rows, :] = total
+                x_out[n] = total.astype(BF16).reshape(4, OWN, RS_W)
+                for d in (2, 1, 3):
+                    to_chip(n, d).start()
+
+        for n in range(N_RS):
+            part[n, rows, :] = jnp.dot(
+                lhs, weight[:, n * RS_W : (n + 1) * RS_W], preferred_element_type=F32
+            )
+
+            @pl.when(c != h)
+            def _():
+                sib_out[n] = part[n, rows, :].astype(BF16)
+                to_sibling(n).start()
+
+            if n > 0:
+                chips(n - 1)
+        chips(N_RS - 1)
+
+        def own(n):
+            total = part[n, pl.ds(my_rows, OWN), :]
+            for d in (1, 3, 2):
+                to_chip(n, d).wait_recv()
+                total = total + x_in[n, d].astype(F32)
+            return total
+
+        def finish():
+            @pl.when(c == h)
+            def _():
+                for n in range(N_RS):
+                    for d in (1, 3, 2):
+                        to_chip(n, d).wait_send()
+
+            @pl.when(c != h)
+            def _():
+                for n in range(N_RS):
+                    to_sibling(n).wait_send()
+
+        return own, finish
+
+    def half_rows(h, k, d):
+        at = pl.ds(pl.multiple_of(64 * h + OWN * add4(x, -d), OWN), OWN)
+        return nrm.at[at, pl.ds(k * AG_W, AG_W)]
+
+    def row_copy(h, k, d, direct):
+        ref = half_rows(h, k, 0 if direct else d)
+        send, recv = (agx_s, agx_r) if direct else (ags_s, ags_r)
+        return pltpu.make_async_remote_copy(
+            src_ref=ref, dst_ref=ref, send_sem=send.at[k, d], recv_sem=recv.at[k, d],
+            device_id=chip(d) if direct else sibling, device_id_type=MESH,
+        )
+
+    def half_finish(h, scattered, complete):
+        own, finish = scattered
+
+        @pl.when(c == h)
+        def _():
+            complete(own)
+            for k in range(N_AG):
+                for d in (2, 1, 3):
+                    row_copy(h, k, d, True).start()
+                row_copy(h, k, 0, False).start()
+
+        finish()
+
+    def half_ready(h):
+        @pl.when(c == h)
+        def _():
+            for k in range(N_AG):
+                for d in (1, 3, 2):
+                    row_copy(h, k, d, True).wait_recv()
+                    row_copy(h, k, d, False).start()
+
+        @pl.when(c != h)
+        def _():
+            for k in range(N_AG):
+                for d in (0, 1, 3, 2):
+                    row_copy(h, k, d, False).wait_recv()
+
+    def half_sent(h):
+        @pl.when(c == h)
+        def _():
+            for k in range(N_AG):
+                for d in (1, 3, 2):
+                    row_copy(h, k, d, True).wait_send()
+                for d in (0, 1, 3, 2):
+                    row_copy(h, k, d, False).wait_send()
+
+    def last_rows(own):
+        for n in range(N_RS):
+            cols = slice(n * RS_W, (n + 1) * RS_W)
+            nrm[pl.ds(my_rows, OWN), cols] = (res[:, cols] + own(n)).astype(BF16)
 
     gather_0()
     tables()
@@ -472,12 +562,12 @@
     res[...] = x_v[pl.ds(my_rows, OWN), :].astype(F32)
     loads["wq"].wait()
     loads["wkv"].wait()
-    project(lambda k: None)
+    project(0, ROWS)
     loads["prompt"].wait()
     loads["cache"].wait()
-    attention()
+    attention(0, ROWS)
     loads["wo"].wait()
-    own, rs_done = reduce_scatter(attended(), wo_v)
+    own, rs_done = reduce_scatter(attended(0, ROWS), wo_v)
     turn(0, 0)
     turn(1, 1)
     turn(1, 0)
@@ -496,54 +586,51 @@
         spread(0, a)
     rows_done()
     sums_done()
-    activate()
+    activate(0, ROWS)
     loads["wd"].wait()
     loads["tok"].wait()
-    own, rs_done = reduce_scatter(hid[...], wd_v)
-    between_passes(own)
-    rs_done()
-
-    ready, ag_done = share_rows()
-    project(ready)
-    ag_done()
+    low, high = (0, 64), (64, 128)
+    sums_0 = half_scatter(0, hid[:64, :], wd_v)
+    sums_1 = half_scatter(1, hid[64:, :], wd_v)
+
+    half_finish(0, sums_0, between_passes)
+    half_finish(1, sums_1, between_passes)
+    half_ready(0)
+    project(*low)
+    half_sent(0)
+    attention(*low)
+    sums_0 = half_scatter(0, attended(*low), wo_v)
+    half_ready(1)
+    project(*high)
+    half_sent(1)
     for a in (-1, 1, 2):
         forward(1, a)
-    attention()
-    own, rs_done = reduce_scatter(attended(), wo_v)
-    for a in (-1, 1):
+    attention(*high)
+    half_finish(0, sums_0, lambda own: after_attention(own, mlp_gain))
+    sums_1 = half_scatter(1, attended(*high), wo_v)
+    for a in (-1, 1, 2):
         forward(0, a)
-    after_attention(own, mlp_gain)
-    rs_done()
-    ready, ag_done = share_rows()
-    forward(0, 2)
+    half_ready(0)
     halves(0, 0, 2)
     for a in (-1, 1, 2):
         halves(0, a, 2)
         halves(1, a, 2)
-    for k in range(N_AG):
-        ready(k)
-        for part_k in range(2):
-            start = k * AG_W + part_k * (AG_W // 2)
-            at = slice(start, start + AG_W // 2)
-            for acc, weight in ((g_acc, gate_v), (u_acc, up_v)):
-                product = jnp.dot(nrm[:, at], weight[at, :], preferred_element_type=F32)
-                if start == 0:
-                    acc[...] = product
-                else:
-                    acc[...] += product
-    ag_done()
+    gate_up(*low)
+    half_sent(0)
+    half_finish(1, sums_1, lambda own: after_attention(own, mlp_gain))
+    sums_0 = half_scatter(0, hid[:64, :], wd_v)
+    half_ready(1)
+    gate_up(*high)
+    half_sent(1)
+    half_finish(0, sums_0, last_rows)
+    sums_1 = half_scatter(1, hid[64:, :], wd_v)
+    half_finish(1, sums_1, last_rows)
+    half_ready(0)
+    half_ready(1)
+    half_sent(0)
+    half_sent(1)
     for copy in sends[0] + sends[1]:
         copy.wait_send()
-    activate()
-    own, rs_done = reduce_scatter(hid[...], wd_v)
-    for n in range(N_RS):
-        cols = slice(n * RS_W, (n + 1) * RS_W)
-        nrm[pl.ds(my_rows, OWN), cols] = (res[:, cols] + own(n)).astype(BF16)
-    rs_done()
-    ready, ag_done = share_rows()
-    for k in range(N_AG):
-        ready(k)
-    ag_done()
     copy = pltpu.make_async_copy(nrm, out, load_sem.at[0])
     copy.start()
     copy.wait()

time: 146 us -> 146 us (level)
  no operation moved by 1% of the time
where the time goes in v3:
time: 146 us
  Pallas kernels  143 us (98%)
  local copies, waits for them, and re-layouts  2.29 us (2%)
    pallas_call x1, Pallas kernels, body(): pl.pallas_call(kernel, out_shape=jax.ShapeDtypeStruct((ROWS, D), BF16), i...  143 us

profile of v3, /device:TPU:1, one launch (start us, length us, event | category | flops | bytes accessed | tf_op | source)
XLA Modules:
  0.0 145.8 jit_solution(14343923425389271709)
XLA Ops:
  0.7 142.9 %two_passes.1 = bf16[128,4096]{1,0:T(8,128)(2,1)} custom-call(s32[1]{0:T(128)S(6)} %copy.18.prompt_len, s32[1,8]{1,0:T(1,128)} %cache_len.1, s32[1,128]{1,0:T(1,128)} %bitcast.9, f32[1,128]{1,0:T(1,128)} %constant.2.clone.frequency, f32[1,4096]{1,0:T(1,128)} %bitcast.7, f32[1,4096]{1,0:T(1,128)} %bitcast.8, bf16[128,4096]{1,0:T(8,128)(2,1)} %blocks.1, ...), custom_call_target="tpu_custom_call" | custom-call | tf_op jit(solution)/shard_map/two_passes/pallas_call | solution.py:650
  143.5 2.3 %copy.19 = bf16[128,4096]{1,0:T(8,128)(2,1)} copy(bf16[128,4096]{1,0:T(8,128)(2,1)} %two_passes.1) | data formatting | bytes 2097152

commit v4 on v2

--- a/solution.py
+++ b/solution.py
@@ -38,7 +38,7 @@
     x_v, tok_v, prm_v, cache_v, wq_v, wkv_v, wo_v, gate_v, up_v, wd_v,
     nrm, qkv, q_s, k_s, v_s, att, g_acc, u_acc, hid,
     part, sib_out, sib_in, x_out, x_in, res, cos, sin,
-    rows_k, far_out, far_in, near_out, near_in,
+    strided, rows_k, far_out, far_in, near_keep, near_out, near_in,
     load_sem, g_send, g_recv, sib_ss, sib_rs, x_ss, x_rs, agx_s, agx_r, ags_s, ags_r,
     ky_s, ky_r, kx_s, kx_r, ks_s, ks_r, far_s, far_r, near_s, near_r,
 ):
@@ -83,7 +83,7 @@
         loads[name] = copy
 
     barrier = pltpu.get_barrier_semaphore()
-    partners = [chip(1), chip(2), chip(3), sibling, plane(0, 1), plane(0, 3), plane(1, 0), plane(3, 0), plane(2, 0)]
+    partners = [chip(1), chip(2), chip(3), sibling, plane(0, 1), plane(0, 3), plane(1, 0), plane(3, 0), plane(2, 0), plane(0, 2)]
     for who in partners:
         pl.semaphore_signal(barrier, inc=1, device_id=who, device_id_type=MESH)
     pl.semaphore_wait(barrier, len(partners))
@@ -131,12 +131,10 @@
         ).wait_recv()
 
     def gather_0():
-        loads["gate"].wait()
-        loads["up"].wait()
-        for axis in (0, 1):
-            for mat in (0, 1):
-                g_start(mat, 0, 0, None, axis, 1)
-                g_start(mat, 0, 0, None, axis, -1)
+        for mat, name in ((0, "gate"), (1, "up")):
+            loads[name].wait()
+            g_start(mat, 0, 0, None, 0, 1)
+            g_start(mat, 0, 0, None, 0, -1)
 
     def turn(mat, axis):
         for step, half in ((1, 0), (-1, 1)):
@@ -203,7 +201,7 @@
         base = HEADS * HEAD_DIM
         k_s[...] = rope(qkv[:, base : base + HEAD_DIM]).reshape(REQS, BLOCK, HEAD_DIM)
         v_s[...] = qkv[:, base + HEAD_DIM :].astype(BF16).reshape(REQS, BLOCK, HEAD_DIM)
-        scale = 1.0 / math.sqrt(HEAD_DIM)
+        scale = math.log2(math.e) / math.sqrt(HEAD_DIM)
         contract = (((1,), (1,)), ((), ()))
 
         def step(j, carry):
@@ -223,9 +221,9 @@
                 jnp.maximum(jnp.max(s_c, -1, keepdims=True), jnp.max(s_p, -1, keepdims=True)),
                 jnp.max(s_b, -1, keepdims=True),
             )
-            e_c = jnp.exp(s_c - top)
-            e_p = jnp.exp(s_p - top)
-            e_b = jnp.exp(s_b - top)
+            e_c = jnp.exp2(s_c - top)
+            e_p = jnp.exp2(s_p - top)
+            e_b = jnp.exp2(s_b - top)
             total = (
                 jnp.sum(e_c, -1, keepdims=True)
                 + jnp.sum(e_p, -1, keepdims=True)
@@ -239,7 +237,7 @@
                 att[j, :, HEAD_DIM * h : HEAD_DIM * (h + 1)] = mixed[BLOCK * h : BLOCK * (h + 1)]
             return carry
 
-        lax.fori_loop(0, REQS, step, 0)
+        lax.fori_loop(0, REQS, step, 0, unroll=2)
 
     pending = []
 
@@ -357,6 +355,9 @@
         gate = g_acc[...]
         hid[...] = (gate / (1.0 + jnp.exp(-gate)) * u_acc[...]).astype(BF16)
 
+    def along(mat, d):
+        return plane(d, 0) if mat == 0 else plane(0, d)
+
     def slice_rows():
         made = {}
 
@@ -366,35 +367,50 @@
             )
             made[key].start()
 
-        def rows_of(k, core, d):
+        def rows_of(mat, k, core, d):
             row = 64 * core + OWN * add4(x, d)
-            return rows_k.at[k, pl.ds(pl.multiple_of(row, OWN), OWN)]
-
-        def chunk(dy):
-            return pl.ds(pl.multiple_of(add4(y, dy) * SLICE, SLICE), SLICE)
-
-        def over_x(k):
+            return rows_k.at[mat, k, pl.ds(pl.multiple_of(row, OWN), OWN)]
+
+        def chunk(mat, d):
+            if mat == 0:
+                at = pl.ds(pl.multiple_of(add4(y, d) * SLICE, SLICE), SLICE)
+                return nrm.at[pl.ds(my_rows, OWN), at]
+            return strided.at[add4(z, d)]
+
+        def over_x(mat, k):
+            ref = rows_of(mat, k, c, 0)
             for d in (2, 1, 3):
-                go(("x", k, d), rows_of(k, c, 0), rows_of(k, c, 0), kx_s.at[k, d], kx_r.at[k, d], chip(d))
-            go(("s", k, 0), rows_of(k, c, 0), rows_of(k, c, 0), ks_s.at[k, 0], ks_r.at[k, 0], sibling)
-
-        for dy in (2, 1, 3):
-            k = (-dy) % 4
-            src = nrm.at[pl.ds(my_rows, OWN), chunk(dy)]
-            go(("y", k), src, rows_of(k, c, 0), ky_s.at[k], ky_r.at[k], plane(dy, 0))
-        rows_k[0, pl.ds(my_rows, OWN), :] = nrm[pl.ds(my_rows, OWN), chunk(0)]
-        over_x(0)
-        for k in (2, 1, 3):
-            made["y", k].wait_recv()
-            over_x(k)
-
-        def ready(k):
+                go(("x", mat, k, d), ref, ref, kx_s.at[mat, k, d], kx_r.at[mat, k, d], chip(d))
+            go(("s", mat, k, 0), ref, ref, ks_s.at[mat, k, 0], ks_r.at[mat, k, 0], sibling)
+
+        for i in range(4):
+            for j in range(4):
+                start = SLICE * j + SHARD * i
+                strided[i, :, SHARD * j : SHARD * (j + 1)] = nrm[
+                    pl.ds(my_rows, OWN), start : start + SHARD
+                ]
+        for d in (2, 1, 3):
+            for mat in (0, 1):
+                k = (-d) % 4
+                go(
+                    ("p", mat, k), chunk(mat, d), rows_of(mat, k, c, 0),
+                    ky_s.at[mat, k], ky_r.at[mat, k], along(mat, d),
+                )
+        for mat in (0, 1):
+            rows_k[mat, 0, pl.ds(my_rows, OWN), :] = chunk(mat, 0)[...]
+        for k in (2, 1, 3, 0):
+            for mat in (0, 1):
+                if k > 0:
+                    made["p", mat, k].wait_recv()
+                over_x(mat, k)
+
+        def ready(mat, k):
             for d in (1, 3, 2):
-                made["x", k, d].wait_recv()
-                ref = rows_of(k, c, -d)
-                go(("s", k, d), ref, ref, ks_s.at[k, d], ks_r.at[k, d], sibling)
+                made["x", mat, k, d].wait_recv()
+                ref = rows_of(mat, k, c, -d)
+                go(("s", mat, k, d), ref, ref, ks_s.at[mat, k, d], ks_r.at[mat, k, d], sibling)
             for d in (0, 1, 3, 2):
-                made["s", k, d].wait_recv()
+                made["s", mat, k, d].wait_recv()
 
         def finish():
             for copy in made.values():
@@ -404,57 +420,71 @@
 
     def slice_gate_up(ready):
         made = []
-        at = pl.ds(pl.multiple_of(y * SLICE, SLICE), SLICE)
-
-        def product(k, mat):
-            return jnp.dot(rows_k[k], full[mat][at, :], preferred_element_type=F32)
-
-        def go(src, dst, send, recv, dy):
+        accs = (g_acc, u_acc)
+        half = ROWS // 2
+
+        def product(mat, k):
+            if mat == 0:
+                at = pl.ds(pl.multiple_of(y * SLICE, SLICE), SLICE)
+                return jnp.dot(rows_k[0, k], gate_v[at, :], preferred_element_type=F32)
+            total = jnp.zeros((ROWS, HIDDEN), F32)
+            for j in range(4):
+                at = pl.ds(pl.multiple_of((4 * j + z) * SHARD, SHARD), SHARD)
+                lhs = rows_k[1, k, :, SHARD * j : SHARD * (j + 1)]
+                total += jnp.dot(lhs, up_v[at, :], preferred_element_type=F32)
+            return total
+
+        def go(src, dst, send, recv, who):
             copy = pltpu.make_async_remote_copy(
-                src_ref=src, dst_ref=dst, send_sem=send, recv_sem=recv,
-                device_id=plane(dy, 0), device_id_type=MESH,
+                src_ref=src, dst_ref=dst, send_sem=send, recv_sem=recv, device_id=who, device_id_type=MESH
             )
             copy.start()
             made.append(copy)
             return copy
 
-        ready(2)
-        far = []
+        far = {}
         for mat in (0, 1):
-            far_out[mat] = product(2, mat).astype(BF16)
-            far.append(
-                go(far_out.at[mat], far_in.at[mat], far_s.at[mat], far_r.at[mat], 1 - 2 * mat)
-            )
+            ready(mat, 2)
+            value = product(mat, 2).astype(BF16)
+            for i in (0, 1):
+                far_out[mat, i] = value[half * i : half * (i + 1)]
+                far[mat, i] = go(
+                    far_out.at[mat, i], far_in.at[mat, i], far_s.at[mat, i], far_r.at[mat, i],
+                    along(mat, 1 - 2 * i),
+                )
         near = []
 
-        def send_near(i, mat, value):
-            near_out[i, mat] = value.astype(BF16)
+        def send_near(i, mat, part_i):
             near.append(
                 go(
-                    near_out.at[i, mat], near_in.at[i, mat],
-                    near_s.at[i, mat], near_r.at[i, mat], 1 - 2 * i,
+                    near_out.at[i, mat, part_i], near_in.at[i, mat, part_i],
+                    near_s.at[i, mat, part_i], near_r.at[i, mat, part_i], along(mat, 1 - 2 * i),
                 )
             )
 
-        ready(1)
-        send_near(0, 1, product(1, 1))
-        ready(3)
-        send_near(1, 0, product(3, 0))
-        value = product(1, 0)
-        far[0].wait_recv()
-        send_near(0, 0, value + far_in[0].astype(F32))
-        value = product(3, 1)
-        far[1].wait_recv()
-        send_near(1, 1, value + far_in[1].astype(F32))
-        ready(0)
-        for mat, acc in ((0, g_acc), (1, u_acc)):
-            acc[...] = product(0, mat)
+        for i in (0, 1):
+            for mat in (0, 1):
+                ready(mat, 1 + 2 * i)
+                value = product(mat, 1 + 2 * i)
+                near_keep[i, mat] = value[half * i : half * (i + 1)]
+                near_out[i, mat, 1 - i] = value[half * (1 - i) : half * (2 - i)].astype(BF16)
+                send_near(i, mat, 1 - i)
+        for i in (0, 1):
+            for mat in (0, 1):
+                far[mat, i].wait_recv()
+                near_out[i, mat, i] = (near_keep[i, mat] + far_in[mat, i].astype(F32)).astype(BF16)
+                send_near(i, mat, i)
+        for mat in (0, 1):
+            ready(mat, 0)
+            accs[mat][...] = product(mat, 0)
 
         def collect():
             for copy in near:
                 copy.wait_recv()
-            for mat, acc in ((0, g_acc), (1, u_acc)):
-                acc[...] += near_in[0, mat].astype(F32) + near_in[1, mat].astype(F32)
+            for mat in (0, 1):
+                for i in (0, 1):
+                    rows = slice(half * i, half * (i + 1))
+                    accs[mat][rows, :] += near_in[0, mat, i].astype(F32) + near_in[1, mat, i].astype(F32)
 
         def finish():
             for copy in made:
@@ -476,24 +506,25 @@
     loads["prompt"].wait()
     loads["cache"].wait()
     attention()
+    for mat in (0, 1):
+        turn(mat, 0)
+    for mat in (0, 1):
+        g_start(mat, 0, 0, None, 1, 1)
+        g_start(mat, 0, 0, None, 1, -1)
     loads["wo"].wait()
     own, rs_done = reduce_scatter(attended(), wo_v)
-    turn(0, 0)
-    turn(1, 1)
-    turn(1, 0)
-    turn(0, 1)
     after_attention(own, mlp_gain)
     rs_done()
     ready, rows_done = slice_rows()
     halves(0, 2, 0)
-    halves(1, 0, 2)
+    halves(1, 2, 0)
     collect, sums_done = slice_gate_up(ready)
-    halves(1, 2, 0)
-    for a in (-1, 1, 2):
-        spread(1, a)
+    for mat in (0, 1):
+        turn(mat, 1)
     collect()
     for a in (-1, 1, 2):
-        spread(0, a)
+        for mat in (0, 1):
+            spread(mat, a)
     rows_done()
     sums_done()
     activate()
@@ -506,18 +537,17 @@
     ready, ag_done = share_rows()
     project(ready)
     ag_done()
-    for a in (-1, 1, 2):
-        forward(1, a)
+    for a in (-1, 1):
+        for mat in (0, 1):
+            forward(mat, a)
     attention()
     own, rs_done = reduce_scatter(attended(), wo_v)
-    for a in (-1, 1):
-        forward(0, a)
+    for mat in (0, 1):
+        forward(mat, 2)
     after_attention(own, mlp_gain)
     rs_done()
     ready, ag_done = share_rows()
-    forward(0, 2)
-    halves(0, 0, 2)
-    for a in (-1, 1, 2):
+    for a in (0, -1, 1, 2):
         halves(0, a, 2)
         halves(1, a, 2)
     for k in range(N_AG):
@@ -593,11 +623,13 @@
             pltpu.VMEM((OWN, D), F32),
             pltpu.VMEM((ROWS, HEAD_DIM), F32),
             pltpu.VMEM((ROWS, HEAD_DIM), F32),
-            pltpu.VMEM((4, ROWS, SLICE), BF16),
-            pltpu.VMEM((2, ROWS, HIDDEN), BF16),
-            pltpu.VMEM((2, ROWS, HIDDEN), BF16),
-            pltpu.VMEM((2, 2, ROWS, HIDDEN), BF16),
-            pltpu.VMEM((2, 2, ROWS, HIDDEN), BF16),
+            pltpu.VMEM((4, OWN, SLICE), BF16),
+            pltpu.VMEM((2, 4, ROWS, SLICE), BF16),
+            pltpu.VMEM((2, 2, ROWS // 2, HIDDEN), BF16),
+            pltpu.VMEM((2, 2, ROWS // 2, HIDDEN), BF16),
+            pltpu.VMEM((2, 2, ROWS // 2, HIDDEN), F32),
+            pltpu.VMEM((2, 2, 2, ROWS // 2, HIDDEN), BF16),
+            pltpu.VMEM((2, 2, 2, ROWS // 2, HIDDEN), BF16),
             dma((10,)),
             dma((2, 20)),
             dma((2, 4, 4, 2)),
@@ -609,16 +641,16 @@
             dma((N_AG, 4)),
             dma((N_AG, 4)),
             dma((N_AG, 4)),
-            dma((4,)),
-            dma((4,)),
-            dma((4, 4)),
-            dma((4, 4)),
-            dma((4, 4)),
-            dma((4, 4)),
-            dma((2,)),
-            dma((2,)),
+            dma((2, 4)),
+            dma((2, 4)),
+            dma((2, 4, 4)),
+            dma((2, 4, 4)),
+            dma((2, 4, 4)),
+            dma((2, 4, 4)),
             dma((2, 2)),
             dma((2, 2)),
+            dma((2, 2, 2)),
+            dma((2, 2, 2)),
         ],
         compiler_params=pltpu.CompilerParams(
             collective_id=0, has_side_effects=True, vmem_limit_bytes=60 * 2**20

time: 146 us -> 138 us (0.945)
  Pallas kernels: 143 us -> 135 us
    pallas_call x1, Pallas kernels: 143 us -> 135 us  [body(): pl.pallas_call(kernel, out_shape=jax.ShapeDtypeStruct((ROWS, D), BF16), i...]
where the time goes in v4:
time: 138 us
  Pallas kernels  135 us (98%)
  local copies, waits for them, and re-layouts  2.29 us (2%)
    pallas_call x1, Pallas kernels, body(): pl.pallas_call(kernel, out_shape=jax.ShapeDtypeStruct((ROWS, D), BF16), i...  135 us

profile of v4, /device:TPU:1, one launch (start us, length us, event | category | flops | bytes accessed | tf_op | source)
XLA Modules:
  0.0 138.3 jit_solution(2513977489933991417)
XLA Ops:
  0.7 135.3 %two_passes.1 = bf16[128,4096]{1,0:T(8,128)(2,1)} custom-call(s32[1]{0:T(128)S(6)} %copy.18.prompt_len, s32[1,8]{1,0:T(1,128)} %cache_len.1, s32[1,128]{1,0:T(1,128)} %bitcast.9, f32[1,128]{1,0:T(1,128)} %constant.2.clone.frequency, f32[1,4096]{1,0:T(1,128)} %bitcast.7, f32[1,4096]{1,0:T(1,128)} %bitcast.8, bf16[128,4096]{1,0:T(8,128)(2,1)} %blocks.1, ...), custom_call_target="tpu_custom_call" | custom-call | tf_op jit(solution)/shard_map/two_passes/pallas_call | solution.py:593
  136.0 2.3 %copy.19 = bf16[128,4096]{1,0:T(8,128)(2,1)} copy(bf16[128,4096]{1,0:T(8,128)(2,1)} %two_passes.1) | data formatting | bytes 2097152

commit v5 on v4

--- a/solution.py
+++ b/solution.py
@@ -78,9 +78,9 @@
             ("tok", token.at[pl.ds(my_rows, OWN)], tok_v),
         ]
     ):
-        copy = pltpu.make_async_copy(src, dst, load_sem.at[i])
-        copy.start()
-        loads[name] = copy
+        loads[name] = pltpu.make_async_copy(src, dst, load_sem.at[i])
+    for name in ("gate", "up", "blocks", "wkv", "wq"):
+        loads[name].start()
 
     barrier = pltpu.get_barrier_semaphore()
     partners = [chip(1), chip(2), chip(3), sibling, plane(0, 1), plane(0, 3), plane(1, 0), plane(3, 0), plane(2, 0), plane(0, 2)]
@@ -150,6 +150,13 @@
         g_wait(mat, a, b, 0)
         g_wait(mat, a, b, 1)
 
+    def own_onward():
+        for mat in (0, 1):
+            halves(mat, 2, 0)
+        for mat in (0, 1):
+            g_start(mat, 0, 0, None, 1, 1)
+            g_start(mat, 0, 0, None, 1, -1)
+
     def forward(mat, a):
         g_wait(mat, a, -1)
         g_start(mat, a, -1, 0, 1, 1)
@@ -160,7 +167,7 @@
         lane = lax.broadcasted_iota(jnp.int32, (BLOCK, HEAD_DIM), 1)
         row = lax.broadcasted_iota(jnp.int32, (BLOCK, HEAD_DIM), 0)
         for j in range(REQS):
-            position = row + (prompt_len[0] + cache_len[0, j])
+            position = row + (prompt_len[0, 0] + cache_len[0, j])
             angle = position.astype(F32) * frequency[...]
             cos[BLOCK * j : BLOCK * (j + 1), :] = jnp.cos(angle)
             sine = jnp.sin(angle)
@@ -216,7 +223,7 @@
             at_c = lax.broadcasted_iota(jnp.int32, s_c.shape, 1)
             at_p = lax.broadcasted_iota(jnp.int32, s_p.shape, 1)
             s_c = jnp.where(at_c < cache_len[0, j], s_c, -1e30)
-            s_p = jnp.where(at_p < prompt_len[0], s_p, -1e30)
+            s_p = jnp.where(at_p < prompt_len[0, 0], s_p, -1e30)
             top = jnp.maximum(
                 jnp.maximum(jnp.max(s_c, -1, keepdims=True), jnp.max(s_p, -1, keepdims=True)),
                 jnp.max(s_b, -1, keepdims=True),
@@ -237,7 +244,7 @@
                 att[j, :, HEAD_DIM * h : HEAD_DIM * (h + 1)] = mixed[BLOCK * h : BLOCK * (h + 1)]
             return carry
 
-        lax.fori_loop(0, REQS, step, 0, unroll=2)
+        lax.fori_loop(0, REQS, step, 0, unroll=4)
 
     pending = []
 
@@ -358,7 +365,7 @@
     def along(mat, d):
         return plane(d, 0) if mat == 0 else plane(0, d)
 
-    def slice_rows():
+    def slice_rows(meanwhile):
         made = {}
 
         def go(key, src, dst, send, recv, who):
@@ -398,11 +405,13 @@
                 )
         for mat in (0, 1):
             rows_k[mat, 0, pl.ds(my_rows, OWN), :] = chunk(mat, 0)[...]
-        for k in (2, 1, 3, 0):
+        for mat in (0, 1):
+            over_x(mat, 0)
+        for k in (2, 1, 3):
             for mat in (0, 1):
-                if k > 0:
-                    made["p", mat, k].wait_recv()
+                made["p", mat, k].wait_recv()
                 over_x(mat, k)
+        meanwhile()
 
         def ready(mat, k):
             for d in (1, 3, 2):
@@ -502,29 +511,25 @@
     res[...] = x_v[pl.ds(my_rows, OWN), :].astype(F32)
     loads["wq"].wait()
     loads["wkv"].wait()
+    for name in ("prompt", "cache", "wo", "wd", "tok"):
+        loads[name].start()
     project(lambda k: None)
     loads["prompt"].wait()
     loads["cache"].wait()
     attention()
+    loads["wo"].wait()
+    own, rs_done = reduce_scatter(attended(), wo_v)
     for mat in (0, 1):
         turn(mat, 0)
-    for mat in (0, 1):
-        g_start(mat, 0, 0, None, 1, 1)
-        g_start(mat, 0, 0, None, 1, -1)
-    loads["wo"].wait()
-    own, rs_done = reduce_scatter(attended(), wo_v)
     after_attention(own, mlp_gain)
     rs_done()
-    ready, rows_done = slice_rows()
-    halves(0, 2, 0)
-    halves(1, 2, 0)
+    ready, rows_done = slice_rows(own_onward)
     collect, sums_done = slice_gate_up(ready)
+    collect()
     for mat in (0, 1):
         turn(mat, 1)
-    collect()
-    for a in (-1, 1, 2):
-        for mat in (0, 1):
-            spread(mat, a)
+        spread(mat, -1)
+        spread(mat, 1)
     rows_done()
     sums_done()
     activate()
@@ -537,16 +542,18 @@
     ready, ag_done = share_rows()
     project(ready)
     ag_done()
-    for a in (-1, 1):
-        for mat in (0, 1):
-            forward(mat, a)
+    for mat in (0, 1):
+        forward(mat, -1)
+        spread(mat, 2)
     attention()
+    for mat in (0, 1):
+        forward(mat, 1)
     own, rs_done = reduce_scatter(attended(), wo_v)
-    for mat in (0, 1):
-        forward(mat, 2)
     after_attention(own, mlp_gain)
     rs_done()
     ready, ag_done = share_rows()
+    for mat in (0, 1):
+        forward(mat, 2)
     for a in (0, -1, 1, 2):
         halves(0, a, 2)
         halves(1, a, 2)
@@ -657,7 +664,7 @@
         ),
         name="two_passes",
     )(
-        prompt_len, cache_len, accepted[None, :], frequency, attn_gain[None, :], mlp_gain[None, :],
+        prompt_len[None, :], cache_len, accepted[None, :], frequency, attn_gain[None, :], mlp_gain[None, :],
         blocks, token_embed, prompt_kv[0], cache_kv[0], w_q, w_kv, w_o, w_gate, w_up, w_down,
     )
 

time: 138 us -> 133 us (0.964)
  Pallas kernels: 135 us -> 130 us
    pallas_call x1, Pallas kernels: 135 us -> 130 us  [body(): pl.pallas_call(kernel, out_shape=jax.ShapeDtypeStruct((ROWS, D), BF16), i...]
where the time goes in v5:
time: 133 us
  Pallas kernels  130 us (98%)
  local copies, waits for them, and re-layouts  2.29 us (2%)
    pallas_call x1, Pallas kernels, body(): pl.pallas_call(kernel, out_shape=jax.ShapeDtypeStruct((ROWS, D), BF16), i...  130 us

profile of v5, /device:TPU:1, one launch (start us, length us, event | category | flops | bytes accessed | tf_op | source)
XLA Modules:
  0.0 132.8 jit_solution(15715363199540591035)
XLA Ops:
  0.7 129.8 %two_passes.1 = bf16[128,4096]{1,0:T(8,128)(2,1)} custom-call(s32[1,1]{1,0:T(1,128)} %bitcast.6.prompt_len, s32[1,8]{1,0:T(1,128)} %cache_len.1, s32[1,128]{1,0:T(1,128)} %bitcast.11, f32[1,128]{1,0:T(1,128)} %constant.2.clone.frequency, f32[1,4096]{1,0:T(1,128)} %bitcast.9, f32[1,4096]{1,0:T(1,128)} %bitcast.10, bf16[128,4096]{1,0:T(8,128)(2,1)} %blocks.1, ...), custom_call_target="tpu_custom_call" | custom-call | tf_op jit(solution)/shard_map/two_passes/pallas_call | solution.py:600
  130.5 2.3 %copy.19 = bf16[128,4096]{1,0:T(8,128)(2,1)} copy(bf16[128,4096]{1,0:T(8,128)(2,1)} %two_passes.1) | data formatting | bytes 2097152

commit v6 on v5

--- a/solution.py
+++ b/solution.py
@@ -554,20 +554,20 @@
     ready, ag_done = share_rows()
     for mat in (0, 1):
         forward(mat, 2)
-    for a in (0, -1, 1, 2):
-        halves(0, a, 2)
-        halves(1, a, 2)
     for k in range(N_AG):
         ready(k)
-        for part_k in range(2):
-            start = k * AG_W + part_k * (AG_W // 2)
-            at = slice(start, start + AG_W // 2)
-            for acc, weight in ((g_acc, gate_v), (u_acc, up_v)):
-                product = jnp.dot(nrm[:, at], weight[at, :], preferred_element_type=F32)
-                if start == 0:
-                    acc[...] = product
-                else:
-                    acc[...] += product
+    for dy in (0, -1, 1, 2):
+        if dy == 2:
+            for a in (0, -1, 1, 2):
+                halves(0, a, 2)
+        halves(1, dy, 2)
+        at = pl.ds(pl.multiple_of(add4(y, dy) * SLICE, SLICE), SLICE)
+        for acc, weight in ((g_acc, gate_v), (u_acc, up_v)):
+            product = jnp.dot(nrm[:, at], weight[at, :], preferred_element_type=F32)
+            if dy == 0:
+                acc[...] = product
+            else:
+                acc[...] += product
     ag_done()
     for copy in sends[0] + sends[1]:
         copy.wait_send()

time: 133 us -> 129 us (0.970)
  Pallas kernels: 130 us -> 126 us
    pallas_call x1, Pallas kernels: 130 us -> 126 us  [body(): pl.pallas_call(kernel, out_shape=jax.ShapeDtypeStruct((ROWS, D), BF16), i...]
where the time goes in v6:
time: 129 us
  Pallas kernels  126 us (98%)
  local copies, waits for them, and re-layouts  2.29 us (2%)
    pallas_call x1, Pallas kernels, body(): pl.pallas_call(kernel, out_shape=jax.ShapeDtypeStruct((ROWS, D), BF16), i...  126 us

profile of v6, /device:TPU:1, one launch (start us, length us, event | category | flops | bytes accessed | tf_op | source)
XLA Modules:
  0.0 128.6 jit_solution(14971146744891224625)
XLA Ops:
  0.7 125.6 %two_passes.1 = bf16[128,4096]{1,0:T(8,128)(2,1)} custom-call(s32[1,1]{1,0:T(1,128)} %bitcast.6.prompt_len, s32[1,8]{1,0:T(1,128)} %cache_len.1, s32[1,128]{1,0:T(1,128)} %bitcast.11, f32[1,128]{1,0:T(1,128)} %constant.2.clone.frequency, f32[1,4096]{1,0:T(1,128)} %bitcast.9, f32[1,4096]{1,0:T(1,128)} %bitcast.10, bf16[128,4096]{1,0:T(8,128)(2,1)} %blocks.1, ...), custom_call_target="tpu_custom_call" | custom-call | tf_op jit(solution)/shard_map/two_passes/pallas_call | solution.py:600
  126.3 2.3 %copy.19 = bf16[128,4096]{1,0:T(8,128)(2,1)} copy(bf16[128,4096]{1,0:T(8,128)(2,1)} %two_passes.1) | data formatting | bytes 2097152
